TPU v7x, 256 devices: a whole 4x4x8 slice. The times are simulated.
256 devices in a mesh: adapter: 64 (over x, z, core), tensor: 4 (over y).
Axes of the slice: x: 4, y: 4, z: 8, core: 2. Of those that a mesh axis runs over, the one named last changes fastest.
Arguments:
- activations: bfloat16 [32768, 4096], P('adapter', 'tensor'), may hold values from -6 to 6
- output_gradient: bfloat16 [32768, 4096], P('adapter', 'tensor'), may hold values from -6 to 6
- frozen_weight: bfloat16 [4096, 4096], P(None, 'tensor'), may hold values from -0.09375 to 0.09375
- adapter_down_weight: bfloat16 [8192, 4096], P('adapter', 'tensor'), may hold values from -0.09375 to 0.09375
- adapter_up_weight: bfloat16 [8192, 4096], P('adapter', 'tensor'), may hold values from -0.09375 to 0.09375
- adapter_slot_table: int32 [512], replicated, may hold values from 0 to 511, as said below
- group_adapter_index: int32 [64, 48], P('adapter'), may hold values from 0 to 511, as said below
- group_token_length: int32 [64, 48], P('adapter'), may hold values from 1 to 16, as said below
Outputs:
- input_gradient: bfloat16 [32768, 4096], P('adapter', 'tensor')
- down_grad: float32 [8192, 4096], P('adapter', 'tensor')
- up_grad: float32 [8192, 4096], P('adapter', 'tensor')
Inputs may be any that keep to these rules, and one draw needn't show every extreme that they name: `adapter_slot_table`: a permutation of the slots; slot k lies on adapter index k // 8. `group_adapter_index`: the adapters of one index's groups lie on distinct indices of the adapter axis; on every index one group of exactly 16 tokens uses an adapter stored on one index that is the same for all indices. `group_token_length`: each row sums to 512 and holds a group of exactly 16 tokens.
All inputs are finite; a program needn't handle non-finite values.
Results may differ from a plain program's by a relative error of at most 0.015.
Values may be sent and summed in bfloat16 or wider, within the bound.
A program may use at most 128 MiB of HBM per device.

v0:
```python
import jax
import jax.numpy as jnp
from jax import lax
from jax.sharding import PartitionSpec as P

ADAPTER_RANK = 16
ADP_DEV = 8


adapter_scale = 2.0


def rank_sums(down_part, up_part):
    return (
        lax.psum(down_part.astype(jnp.bfloat16), "tensor").astype(jnp.float32),
        lax.psum(up_part.astype(jnp.bfloat16), "tensor").astype(jnp.float32),
    )


def widen(mask, values):
    return jnp.where(mask[:, :, None], values[:, None, :], jnp.zeros((), values.dtype)).reshape(
        values.shape[0], mask.shape[1] * values.shape[1]
    )


def narrow(wide, mask):
    shaped = wide.reshape(wide.shape[0], mask.shape[1], ADAPTER_RANK)
    return jnp.sum(shaped * mask[:, :, None].astype(jnp.float32), axis=1)


def on_device(
    activations,
    output_gradient,
    frozen_weight,
    adapter_down_weight,
    adapter_up_weight,
    adapter_slot_table,
    group_adapter_index,
    group_token_length,
):
    tok_rows = activations.shape[0]
    devices = lax.axis_size("adapter")
    own_index = lax.axis_index("adapter")
    adapter_count = adapter_slot_table.shape[0]
    lengths = group_token_length[0]
    matched = group_adapter_index[0][:, None] == jnp.arange(adapter_count, dtype=jnp.int32)[None, :]
    group_slot = jnp.sum(jnp.where(matched, adapter_slot_table[None, :], 0), axis=1)
    group_owner = group_slot // ADP_DEV
    group_end = jnp.cumsum(lengths)
    positions = jnp.arange(tok_rows, dtype=jnp.int32)
    tok_group = jnp.sum((positions[:, None] >= group_end[None, :]).astype(jnp.int32), axis=1)
    group_onehot = tok_group[:, None] == jnp.arange(lengths.shape[0], dtype=jnp.int32)[None, :]
    tok_owner = jnp.sum(jnp.where(group_onehot, group_owner[None, :], 0), axis=1)
    gathered = lax.all_gather(jnp.stack([group_slot, lengths])[None], "adapter", axis=0, tiled=True)
    from_mine = gathered[:, 0] // ADP_DEV == own_index
    source_count = jnp.sum(jnp.where(from_mine, gathered[:, 1], 0), axis=1)
    source_local = jnp.sum(jnp.where(from_mine, gathered[:, 0] % ADP_DEV, 0), axis=1)
    source_hot = (source_local[:, None] == jnp.arange(ADP_DEV, dtype=jnp.int32)[None, :]) & (
        source_count > 0
    )[:, None]
    eye_rank = jnp.eye(ADAPTER_RANK, dtype=bool)
    selector = (source_hot[:, None, :, None] & eye_rank[None, :, None, :]).reshape(
        devices * ADAPTER_RANK, ADP_DEV * ADAPTER_RANK
    )
    selected_reduced = selector.astype(jnp.bfloat16)
    outgoing_down = jnp.dot(
        selected_reduced, adapter_down_weight, preferred_element_type=jnp.float32
    ).astype(jnp.bfloat16)
    outgoing_up = jnp.dot(
        selected_reduced, adapter_up_weight, preferred_element_type=jnp.float32
    ).astype(jnp.bfloat16)
    received_down, got_up = (
        lax.all_to_all(outgoing_down, "adapter", split_axis=0, concat_axis=0, tiled=True),
        lax.all_to_all(outgoing_up, "adapter", split_axis=0, concat_axis=0, tiled=True),
    )
    owner_hot = tok_owner[:, None] == jnp.arange(devices, dtype=jnp.int32)[None, :]
    down_wide = lax.dot_general(
        activations, received_down, (((1,), (1,)), ((), ())), preferred_element_type=jnp.float32
    )
    up_wide = lax.dot_general(
        output_gradient, got_up, (((1,), (1,)), ((), ())), preferred_element_type=jnp.float32
    )
    down_proj, up_proj = rank_sums(narrow(down_wide, owner_hot), narrow(up_wide, owner_hot))
    down_spread = widen(owner_hot, down_proj.astype(jnp.bfloat16))
    up_broadcast = widen(owner_hot, up_proj.astype(jnp.bfloat16))
    adapter_term = (
        adapter_scale * jnp.dot(up_broadcast, received_down, preferred_element_type=jnp.float32)
    ).astype(jnp.bfloat16)
    partial_down = adapter_scale * lax.dot_general(
        up_broadcast, activations, (((0,), (0,)), ((), ())), preferred_element_type=jnp.float32
    )
    partial_up = adapter_scale * lax.dot_general(
        down_spread, output_gradient, (((0,), (0,)), ((), ())), preferred_element_type=jnp.float32
    )
    back_down, back_up = (
        lax.all_to_all(
            partial_down.astype(jnp.bfloat16), "adapter", split_axis=0, concat_axis=0, tiled=True
        ).astype(partial_down.dtype),
        lax.all_to_all(
            partial_up.astype(jnp.bfloat16), "adapter", split_axis=0, concat_axis=0, tiled=True
        ).astype(partial_up.dtype),
    )
    select_full = selector.astype(jnp.float32)
    down_grad = lax.dot_general(
        select_full,
        back_down,
        (((0,), (0,)), ((), ())),
        precision=lax.Precision.HIGHEST,
        preferred_element_type=jnp.float32,
    )
    up_grad = lax.dot_general(
        select_full,
        back_up,
        (((0,), (0,)), ((), ())),
        precision=lax.Precision.HIGHEST,
        preferred_element_type=jnp.float32,
    )
    frozen_total_sum = lax.psum_scatter(
        lax.dot_general(
            frozen_weight,
            output_gradient,
            (((1,), (1,)), ((), ())),
            preferred_element_type=jnp.float32,
        ).astype(jnp.bfloat16),
        "tensor",
        scatter_dimension=0,
        tiled=True,
    ).astype(jnp.float32)
    input_gradient = (frozen_total_sum.T + adapter_term.astype(jnp.float32)).astype(jnp.bfloat16)
    return (input_gradient, down_grad, up_grad)


def solution(mesh):
    in_specs = (
        P("adapter", "tensor"),
        P("adapter", "tensor"),
        P(None, "tensor"),
        P("adapter", "tensor"),
        P("adapter", "tensor"),
        P(),
        P("adapter", None),
        P("adapter", None),
    )
    out_specs = (P("adapter", "tensor"), P("adapter", "tensor"), P("adapter", "tensor"))
    return jax.shard_map(
        on_device, mesh=mesh, in_specs=in_specs, out_specs=out_specs, check_vma=False
    )
```

profile of v0, /device:TPU:8, one launch (start us, length us, event | category | flops | bytes accessed | tf_op | source)
XLA Modules:
  0.0 327.0 jit_solution(9683461043637806220)
XLA Ops:
  7.2 1.0 select_reduce_fusion.1
  8.8 46.8 %all-gather.1 = s32[64,2,48]{2,1,0:T(2,128)S(1)} all-gather(s32[1,2,48]{2,1,0:T(2,128)S(1)} %add_bitcast_fusion), channel_id=2, replica_groups=mesh['adapter'=64,'tensor'=4] {'adapter'}, dimensions={0}, use_global_device_ids=true | all-gather | bytes 24960 | tf_op jit(solution)/shard_map/all_gather | solution.py:54
  56.5 1.5 and.72
  58.0 2.0 convolution_convert_fusion.1
  60.0 6.9 %all-to-all-start.1 = ((bf16[64,16,1024]{2,1,0:T(8,128)(2,1)}), bf16[64,16,1024]{2,1,0:T(8,128)(2,1)S(1)}, u32[]{:S(2)}, u32[]{:S(2)}) async-start(bf16[64,16,1024]{2,1,0:T(8,128)(2,1)} %bitcast.11), calls=%async_computation.2 | async-start | bytes 4194304 | tf_op jit(solution)/shard_map/all_to_all | solution.py:73
  66.9 2.0 convolution_convert_fusion.2
  68.9 49.1 %all-to-all-done.1 = bf16[64,16,1024]{2,1,0:T(8,128)(2,1)S(1)} async-done(((bf16[64,16,1024]{2,1,0:T(8,128)(2,1)}), bf16[64,16,1024]{2,1,0:T(8,128)(2,1)S(1)}, u32[]{:S(2)}, u32[]{:S(2)}) %all-to-all-start.1) | async-done | bytes 2097184 | tf_op jit(solution)/shard_map/all_to_all | solution.py:73
  118.1 6.3 %all-to-all-start = ((bf16[64,16,1024]{2,1,0:T(8,128)(2,1)}), bf16[64,16,1024]{2,1,0:T(8,128)(2,1)}, u32[]{:S(2)}, u32[]{:S(2)}) async-start(bf16[64,16,1024]{2,1,0:T(8,128)(2,1)} %bitcast.7), calls=%async_computation.1 | async-start | bytes 4194304 | tf_op jit(solution)/shard_map/all_to_all | solution.py:74
  124.9 3.9 %fusion.13 = f32[1024,512]{1,0:T(8,128)} fusion(bf16[1024,1024]{1,0:T(8,128)(2,1)S(1)} %bitcast.57, bf16[512,1024]{1,0:T(8,128)(2,1)} %param.8), kind=kOutput, calls=%fused_computation.47 | convolution fusion | flops 1073741824 | bytes 5242880 | tf_op jit(solution)/shard_map/dot_general | solution.py:77
  128.8 46.6 %all-to-all-done = bf16[64,16,1024]{2,1,0:T(8,128)(2,1)} async-done(((bf16[64,16,1024]{2,1,0:T(8,128)(2,1)}), bf16[64,16,1024]{2,1,0:T(8,128)(2,1)}, u32[]{:S(2)}, u32[]{:S(2)}) %all-to-all-start) | async-done | bytes 2097184 | tf_op jit(solution)/shard_map/all_to_all | solution.py:74
  175.4 3.0 fusion.11
  179.1 14.3 %all-reduce = (bf16[512,16]{0,1:T(8,128)(2,1)S(1)}, bf16[512,16]{0,1:T(8,128)(2,1)S(1)}) all-reduce(bf16[512,16]{0,1:T(8,128)(2,1)S(1)} %get-tuple-element.16, bf16[512,16]{0,1:T(8,128)(2,1)S(1)} %get-tuple-element.15), channel_id=1, replica_groups=mesh['adapter'=64,'tensor'=4] {'tensor'}, use_global_device_ids=true, to_apply=%region_8.9 | all-reduce | flops 16384 | bytes 65536 | tf_op jit(solution)/shard_map/psum | solution.py:16
  193.4 1.2 broadcast_select_fusion
  194.6 2.6 multiply_convert_fusion
  197.2 5.9 %all-to-all-start.3 = ((bf16[64,16,1024]{2,1,0:T(8,128)(2,1)}), bf16[64,16,1024]{2,1,0:T(8,128)(2,1)S(1)}, u32[]{:S(2)}, u32[]{:S(2)}) async-start(bf16[64,16,1024]{2,1,0:T(8,128)(2,1)} %bitcast.58), calls=%async_computation.4 | async-start | bytes 4194304 | tf_op jit(solution)/shard_map/all_to_all | solution.py:99
  203.3 9.6 %convolution_convert_fusion = bf16[4096,512]{1,0:T(8,128)(2,1)} fusion(bf16[4096,1024]{1,0:T(8,128)(2,1)} %param.10, bf16[512,1024]{1,0:T(8,128)(2,1)S(1)} %copy-done), kind=kOutput, calls=%fused_computation | convolution fusion | flops 4297064448 | bytes 13631488 | tf_op jit(solution)/shard_map/dot_general | solution.py:119
  212.9 4.2 %multiply_convert_fusion.1 = bf16[1024,1024]{1,0:T(8,128)(2,1)} fusion(bf16[512,1024]{0,1:T(8,128)(2,1)} %bitcast.62, bf16[512,1024]{1,0:T(8,128)(2,1)} %param.8), kind=kOutput, calls=%fused_computation.2 | convolution fusion | flops 1075838976 | bytes 4194304 | tf_op jit(solution)/shard_map/dot_general | solution.py:89
  217.1 37.2 %all-to-all-done.3 = bf16[64,16,1024]{2,1,0:T(8,128)(2,1)S(1)} async-done(((bf16[64,16,1024]{2,1,0:T(8,128)(2,1)}), bf16[64,16,1024]{2,1,0:T(8,128)(2,1)S(1)}, u32[]{:S(2)}, u32[]{:S(2)}) %all-to-all-start.3) | async-done | bytes 2097184 | tf_op jit(solution)/shard_map/all_to_all | solution.py:99
  254.3 6.1 %all-to-all-start.2 = ((bf16[64,16,1024]{2,1,0:T(8,128)(2,1)}), bf16[64,16,1024]{2,1,0:T(8,128)(2,1)}, u32[]{:S(2)}, u32[]{:S(2)}) async-start(bf16[64,16,1024]{2,1,0:T(8,128)(2,1)} %bitcast.59), calls=%async_computation.3 | async-start | bytes 4194304 | tf_op jit(solution)/shard_map/all_to_all | solution.py:96
  260.4 1.3 fusion.14
  261.7 49.7 %all-to-all-done.2 = bf16[64,16,1024]{2,1,0:T(8,128)(2,1)} async-done(((bf16[64,16,1024]{2,1,0:T(8,128)(2,1)}), bf16[64,16,1024]{2,1,0:T(8,128)(2,1)}, u32[]{:S(2)}, u32[]{:S(2)}) %all-to-all-start.2) | async-done | bytes 2097184 | tf_op jit(solution)/shard_map/all_to_all | solution.py:96
  311.4 2.9 fusion.12
  314.3 3.5 %fusion.1 = bf16[512,1024]{0,1:T(8,128)(2,1)} fusion(bf16[1024,512]{1,0:T(8,128)(2,1)} %reduce-scatter.2.cloned.1.call-done, bf16[64,16,1024]{2,1,0:T(8,128)(2,1)S(1)} %copy-done.2, pred[512,64]{0,1:T(8,128)(4,1)S(1)} %get-tuple-element.26, bf16[512,16]{0,1:T(8,128)(2,1)S(1)} %get-tuple-element.19), kind=kOutput, calls=%fused_computation.6 | convolution fusion | flops 1077411840 | bytes 4243456 | tf_op jit(solution)/shard_map/dot_general | solution.py:87
  317.9 2.3 copy.30
  (32 shorter events, 3.0 us)
Async XLA Ops:
  7.2 168.2 %copy-start = (bf16[512,1024]{1,0:T(8,128)(2,1)S(1)}, bf16[512,1024]{1,0:T(8,128)(2,1)}, u32[]{:S(2)}) copy-start(bf16[512,1024]{1,0:T(8,128)(2,1)} %param.9) | copy-start | bytes 3145732
  7.2 50.8 %copy-start.4 = (bf16[128,1024]{1,0:T(8,128)(2,1)S(1)}, bf16[128,1024]{1,0:T(8,128)(2,1)}, u32[]{:S(2)}) copy-start(bf16[128,1024]{1,0:T(8,128)(2,1)} %param.11) | copy-start | bytes 786436
  60.0 6.9 %copy-start.5 = (bf16[128,1024]{1,0:T(8,128)(2,1)S(1)}, bf16[128,1024]{1,0:T(8,128)(2,1)}, u32[]{:S(2)}) copy-start(bf16[128,1024]{1,0:T(8,128)(2,1)} %param.12) | copy-start | bytes 786436
  60.0 58.1 %all-to-all-start.1 = ((bf16[64,16,1024]{2,1,0:T(8,128)(2,1)}), bf16[64,16,1024]{2,1,0:T(8,128)(2,1)S(1)}, u32[]{:S(2)}, u32[]{:S(2)}) async-start(bf16[64,16,1024]{2,1,0:T(8,128)(2,1)} %bitcast.11), calls=%async_computation.2 | async-start | bytes 4194304 | tf_op jit(solution)/shard_map/all_to_all | solution.py:73
  118.1 6.8 %copy-start.1 = (bf16[64,16,1024]{2,1,0:T(8,128)(2,1)}, bf16[64,16,1024]{2,1,0:T(8,128)(2,1)S(1)}, u32[]{:S(2)}) copy-start(bf16[64,16,1024]{2,1,0:T(8,128)(2,1)S(1)} %all-to-all-done.1) | copy-start | bytes 6291460
  118.1 6.3 %copy-start.6 = (s32[1,48]{1,0:T(1,128)S(1)}, s32[1,48]{1,0:T(1,128)}, u32[]{:S(2)}) copy-start(s32[1,48]{1,0:T(1,128)} %param.15) | copy-start | bytes 580
  118.1 57.3 %all-to-all-start = ((bf16[64,16,1024]{2,1,0:T(8,128)(2,1)}), bf16[64,16,1024]{2,1,0:T(8,128)(2,1)}, u32[]{:S(2)}, u32[]{:S(2)}) async-start(bf16[64,16,1024]{2,1,0:T(8,128)(2,1)} %bitcast.7), calls=%async_computation.1 | async-start | bytes 4194304 | tf_op jit(solution)/shard_map/all_to_all | solution.py:74
  175.4 3.0 copy-start.3
  197.2 57.1 %all-to-all-start.3 = ((bf16[64,16,1024]{2,1,0:T(8,128)(2,1)}), bf16[64,16,1024]{2,1,0:T(8,128)(2,1)S(1)}, u32[]{:S(2)}, u32[]{:S(2)}) async-start(bf16[64,16,1024]{2,1,0:T(8,128)(2,1)} %bitcast.58), calls=%async_computation.4 | async-start | bytes 4194304 | tf_op jit(solution)/shard_map/all_to_all | solution.py:99
  203.1 111.2 %reduce-scatter.2.cloned.1.call-start = ((), (), s32[]{:S(2)}) async-start(), calls=%async_computation.5 | async-start | bytes 5242880 | tf_op jit(solution)/shard_map/reduce_scatter | solution.py:118
  254.3 57.2 %all-to-all-start.2 = ((bf16[64,16,1024]{2,1,0:T(8,128)(2,1)}), bf16[64,16,1024]{2,1,0:T(8,128)(2,1)}, u32[]{:S(2)}, u32[]{:S(2)}) async-start(bf16[64,16,1024]{2,1,0:T(8,128)(2,1)} %bitcast.59), calls=%async_computation.3 | async-start | bytes 4194304 | tf_op jit(solution)/shard_map/all_to_all | solution.py:96
  261.7 52.6 %copy-start.2 = (bf16[64,16,1024]{2,1,0:T(8,128)(2,1)S(1)}, bf16[64,16,1024]{2,1,0:T(8,128)(2,1)}, u32[]{:S(2)}) copy-start(bf16[64,16,1024]{2,1,0:T(8,128)(2,1)} %copy-done.1) | copy-start | bytes 6291460
Sparse Core Ops, SparseCore 0:
  213.0 50.6 reduce-scatter.1
where the time goes:
time: 332 us; the launch traced here: 327 us
  waiting for transfers between devices  183 us (55%)
  blocking collectives  61.1 us (18%)
  matrix products  35 us (11%)
  starting transfers between devices  25.4 us (8%)
  between operations  14.2 us (4%)
  other arithmetic  4.68 us (1%)
  local copies, waits for them, and re-layouts  3.91 us (1%)
    all_to_all x1, waiting for transfers between devices, on_device(): lax.all_to_all(partial_down.astype(jnp.bfloat16), 'adapter', split_axis=0...  49.7 us
    all_to_all x1, waiting for transfers between devices, on_device(): lax.all_to_all(outgoing_down, 'adapter', split_axis=0, concat_axis=0, til...  49.1 us
    all_gather x1, blocking collectives, on_device(): lax.all_gather(jnp.stack([group_slot, lengths])[None], 'adapter', axis=0,...  46.8 us
    all_to_all x1, waiting for transfers between devices, on_device(): lax.all_to_all(outgoing_up, 'adapter', split_axis=0, concat_axis=0, tiled...  46.6 us
    all_to_all x1, waiting for transfers between devices, on_device(): lax.all_to_all(partial_up.astype(jnp.bfloat16), 'adapter', split_axis=0,...  37.2 us
    psum x1, blocking collectives, rank_sums(): lax.psum(up_part.astype(jnp.bfloat16), 'tensor').astype(jnp.float32)  14.3 us
    dot_general x1, matrix products, on_device(): lax.dot_general(frozen_weight, output_gradient, (((1,), (1,)), ((), ())),...  9.56 us
    all_to_all x1, starting transfers between devices, on_device(): lax.all_to_all(outgoing_down, 'adapter', split_axis=0, concat_axis=0, til...  6.88 us
  transfers between devices with their start and end apart: 5, of which 4 were waited for; matrix products, arithmetic and copies ran while one was open for 7% of the time, Pallas kernels for 0%

commit v1 on v0

v1 whole, which is shorter than its diff:
```python
import functools

import jax
import jax.numpy as jnp
from jax import lax
from jax.experimental import pallas as pl
from jax.experimental.pallas import tpu as pltpu
from jax.sharding import PartitionSpec as P

MESH = pl.DeviceIdType.MESH
F32 = jnp.float32
BF16 = jnp.bfloat16
RANK = 16
SLOTS = 8
NX, NZ, NC, NY = 4, 8, 2, 4
PLANE = NX * NC
CAP = 16
ROWS = PLANE * CAP
HALF = ROWS // 2
PEERS = ((2, 0), (2, 1), (1, 0), (1, 1), (3, 0), (3, 1), (0, 1))
DIRS = (1, NZ - 1)
HOPS = NZ // 2

NT = (((1,), (1,)), ((), ()))
NN = (((1,), (0,)), ((), ()))


def mm(a, b, dims=NN):
    return lax.dot_general(a, b, dims, preferred_element_type=F32)


def iota(shape, dim):
    return lax.broadcasted_iota(jnp.int32, shape, dim)


def kernel(
    x_hbm, g_hbm, w_hbm, ad_hbm, bu_hbm, table_ref, gai_ref, len_ref,
    dx_ref, dgrad_ref, ugrad_ref,
    xv, gv, wv, xp, gp, tokx, tokg, aga, agb, meta_s, meta_r, masks,
    low_s, low_r, wide, wide_t, base_s, base_r, lora_s, lora_r, rs_s, rs_r, idx_row, idx_col,
    local_sem, x_send, x_recv, ag_send, ag_recv, rs_send, rs_recv, low_send, low_recv, base_send, base_recv,
):
    me = lax.axis_index("adapter")
    y = lax.axis_index("tensor")
    x = lax.div(me, NZ * NC)
    z = lax.rem(lax.div(me, NC), NZ)
    c = lax.rem(me, NC)
    p = x * NC + c

    def at(xx, zz, cc):
        return (xx * NZ + zz) * NC + cc

    def zplus(d):
        return lax.rem(z + (d + 2 * NZ), NZ)

    def column(k):
        dx, dc = k
        return lax.rem(x + dx, NX), lax.rem(c + dc, NC)

    def column_from(k):
        dx, dc = k
        return lax.rem(x + (NX - dx), NX), lax.rem(c + dc, NC)

    locals_ = {
        "g": pltpu.make_async_copy(g_hbm, gv, local_sem.at[0]),
        "x": pltpu.make_async_copy(x_hbm, xv, local_sem.at[1]),
        "b": pltpu.make_async_copy(bu_hbm, agb.at[z], local_sem.at[2]),
        "a": pltpu.make_async_copy(ad_hbm, aga.at[z], local_sem.at[3]),
        "w": pltpu.make_async_copy(w_hbm, wv, local_sem.at[4]),
    }

    def plane_copy(unit, i, src, dst):
        xx, cc = column(PEERS[i])
        return pltpu.make_async_remote_copy(
            src_ref=src, dst_ref=dst, send_sem=x_send.at[unit, i], recv_sem=x_recv.at[unit, i],
            device_id=(at(xx, z, cc), y), device_id_type=MESH,
        )

    def token_copy(unit, i):
        packed, landed = ((gp, tokg), (xp, tokx))[unit]
        xx, cc = column(PEERS[i])
        return plane_copy(unit, i, packed.at[xx * NC + cc], landed.at[:, p])

    def meta_copy(i):
        xx, cc = column(PEERS[i])
        return plane_copy(3, i, meta_s.at[xx * NC + cc], meta_r.at[p])

    def lora_copy(i):
        xx, cc = column(PEERS[i])
        return plane_copy(2, i, lora_s.at[:, xx * NC + cc], lora_r.at[p])

    def ag_copy(u, d, h, f):
        own = (bu_hbm, ad_hbm)[u]
        buf = (agb, aga)[u]
        rows = pl.ds(f * HALF, HALF)
        source = zplus(-(h - 1) if d == 0 else h - 1)
        src = own.at[rows] if h == 1 else buf.at[source, rows]
        return pltpu.make_async_remote_copy(
            src_ref=src, dst_ref=buf.at[source, rows],
            send_sem=ag_send.at[u, d, h - 1, f], recv_sem=ag_recv.at[u, d, h - 1, f],
            device_id=(at(x, zplus(DIRS[d]), c), y), device_id_type=MESH,
        )

    def rs_copy(u, d, h, f):
        return pltpu.make_async_remote_copy(
            src_ref=rs_s.at[u, d, h - 1, f], dst_ref=rs_r.at[u, d, h - 1, f],
            send_sem=rs_send.at[u, d, h - 1, f], recv_sem=rs_recv.at[u, d, h - 1, f],
            device_id=(at(x, zplus(DIRS[d]), c), y), device_id_type=MESH,
        )

    def low_copy(u, dy):
        return pltpu.make_async_remote_copy(
            src_ref=low_s.at[u], dst_ref=low_r.at[u, dy - 1],
            send_sem=low_send.at[u, dy - 1], recv_sem=low_recv.at[u, dy - 1],
            device_id=(me, lax.rem(y + dy, NY)), device_id_type=MESH,
        )

    def base_copy(dy):
        return pltpu.make_async_remote_copy(
            src_ref=base_s.at[dy], dst_ref=base_r.at[dy - 1],
            send_sem=base_send.at[dy - 1], recv_sem=base_recv.at[dy - 1],
            device_id=(me, lax.rem(y + dy, NY)), device_id_type=MESH,
        )

    def halves(h):
        return [(d, f) for f in (0, 1) for d in (0, 1) if h < HOPS or f == d]

    for name in ("g", "b", "x", "w", "a"):
        locals_[name].start()
    barrier = pltpu.get_barrier_semaphore()
    partners = [(at(*_xzc(column(k), z)), y) for k in PEERS]
    partners += [(at(x, zplus(d), c), y) for d in DIRS]
    partners += [(me, lax.rem(y + dy, NY)) for dy in range(1, NY)]
    for partner in partners:
        pl.semaphore_signal(barrier, inc=1, device_id=partner, device_id_type=MESH)

    ng = gai_ref.shape[1]
    toks = gv.shape[0]
    eye = iota((ng, ng), 0) == iota((ng, ng), 1)

    def to_col(row):
        return jnp.sum(jnp.where(eye, row, 0.0), axis=1, keepdims=True)

    def to_row(col):
        return jnp.sum(jnp.where(eye, col, 0.0), axis=0, keepdims=True)

    gai_col = to_col(gai_ref[...].astype(F32)).astype(jnp.int32)
    len_row = len_ref[...].astype(F32)
    len_col = to_col(len_row)
    n_adapters = table_ref.shape[1]
    slot = jnp.sum(
        jnp.where(iota((ng, n_adapters), 1) == gai_col, table_ref[...].astype(F32), 0.0), axis=1, keepdims=True
    ).astype(jnp.int32)
    local = slot & (SLOTS - 1)
    owner_c = (slot >> 3) & 1
    owner_z = (slot >> 4) & (NZ - 1)
    owner_x = slot >> 7
    pair = (owner_x * NC + owner_c) * NZ + owner_z
    start = jnp.sum(jnp.where(iota((ng, ng), 1) < iota((ng, ng), 0), len_row, 0.0), axis=1, keepdims=True)
    shift = (pair * CAP).astype(F32) - start
    end = start + len_col
    t_row = iota((ng, toks), 1).astype(F32)
    idx_row[...] = jnp.sum(
        jnp.where((t_row >= start) & (t_row < end), shift + t_row, 0.0), axis=0, keepdims=True
    ).astype(jnp.int32)
    t_col = iota((toks, ng), 0).astype(F32)
    idx_col[...] = jnp.sum(
        jnp.where((t_col >= to_row(start)) & (t_col < to_row(end)), to_row(shift) + t_col, 0.0), axis=1, keepdims=True
    ).astype(jnp.int32)
    pairs = PLANE * NZ
    slot_of_pair = jnp.sum(
        jnp.where(iota((pairs, ng), 0) == to_row(pair.astype(F32)).astype(jnp.int32), to_row(local.astype(F32)) + 1.0, 0.0),
        axis=1, keepdims=True,
    ).astype(jnp.int32)
    mask = jnp.where((iota((pairs, ROWS), 1) >> 4) + 1 == slot_of_pair, 1.0, 0.0)
    meta_s[...] = mask.reshape(PLANE, NZ, ROWS)
    meta_r[pl.ds(p, 1)] = meta_s[pl.ds(p, 1)]

    pl.semaphore_wait(barrier, len(partners))

    for d, f in halves(1):
        ag_copy(0, d, 1, f).start()
    for i in range(len(PEERS)):
        meta_copy(i).start()

    def pack(source, packed, q):
        hot = jnp.where(iota((ROWS, toks), 0) + q * ROWS == idx_row[...], 1.0, 0.0).astype(BF16)
        packed[q] = mm(hot, source[...]).astype(BF16).reshape(NZ, CAP, -1)

    def forward(u, h):
        for d, f in halves(h):
            source = zplus(-h if d == 0 else h)
            buf = (agb, aga)[u]
            landed = buf.at[source, pl.ds(f * HALF, HALF)]
            pltpu.make_async_remote_copy(
                src_ref=landed, dst_ref=landed, send_sem=ag_send.at[u, d, h - 1, f],
                recv_sem=ag_recv.at[u, d, h - 1, f], device_id=(at(x, zplus(DIRS[d]), c), y), device_id_type=MESH,
            ).wait_recv()
            if h < HOPS and (d, f) in halves(h + 1):
                ag_copy(u, d, h + 1, f).start()

    def base_block(dy):
        block = lax.rem(y + dy, NY)
        width = 256

        def tile(n, carry):
            rows = pl.ds(pl.multiple_of(block * wv.shape[1] + n * width, width), width)
            cols = pl.ds(pl.multiple_of(n * width, width), width)
            base_s[dy, :, cols] = mm(gv[...], wv[rows, :], NT).astype(BF16)
            return carry

        lax.fori_loop(0, wv.shape[1] // width, tile, 0)

    def select(zt, transposed):
        a, b = iota((ROWS, ROWS), 0), iota((ROWS, ROWS), 1)
        narrow, broad = (a, b) if transposed else (b, a)
        return jnp.where(narrow == zt * RANK + (broad & (RANK - 1)), 1.0, 0.0).astype(BF16)

    def project(u, tok, weights):
        def block(zt, acc):
            wide_p = mm(tok[zt].reshape(ROWS, -1), weights[zt], NT) * masks[zt]
            return acc + mm(wide_p.astype(BF16), select(zt, False))

        acc = lax.fori_loop(0, NZ, block, jnp.zeros((ROWS, ROWS), F32))
        low_s[u] = acc.astype(BF16)
        for dy in (2, 1, 3):
            low_copy(u, dy).start()

    def spread(u):
        total = low_s[u].astype(F32)
        for dy in range(1, NY):
            low_copy(u, dy).wait_recv()
            total = total + low_r[u, dy - 1].astype(F32)
        low = total.astype(BF16)

        def block(zt, carry):
            twice = mm(low, select(zt, True)) * (2.0 * masks[zt])
            if u == 0:
                wide[zt] = twice.astype(BF16)
            wide_t[u, zt] = twice.T.astype(BF16)
            return carry

        lax.fori_loop(0, NZ, block, 0)

    def lora(zt):
        lora_s[zt] = mm(wide[zt], aga[zt]).astype(BF16).reshape(PLANE, CAP, -1)

    toks_of = (tokx, tokg)

    def term(u, zt, f):
        return mm(wide_t[u, zt, f * HALF : (f + 1) * HALF, :], toks_of[u][zt].reshape(ROWS, -1))

    def rs_target(d, h):
        return zplus((HOPS + 1 - h) if d == 0 else -(HOPS + 1 - h))

    def rs_init(u):
        for h in (1, 2):
            for d in (0, 1):
                f = d if h == 1 else 1 - d
                rs_s[u, d, h - 1, f] = term(u, rs_target(d, h), f).astype(BF16)
                rs_copy(u, d, h, f).start()

    def rs_step(u, h):
        for f in (0, 1):
            for d in (0, 1):
                if h == 1 and f != d:
                    continue
                rs_copy(u, d, h, f).wait_recv()
                total = rs_r[u, d, h - 1, f].astype(F32) + term(u, rs_target(d, h + 1), f)
                rs_s[u, d, h, f] = total.astype(BF16)
                rs_copy(u, d, h + 1, f).start()

    def rs_last(u):
        out = (dgrad_ref, ugrad_ref)[u]
        for f in (0, 1):
            total = term(u, z, f)
            for d in (0, 1):
                rs_copy(u, d, HOPS, f).wait_recv()
                total = total + rs_r[u, d, HOPS - 1, f].astype(F32)
            out[f * HALF : (f + 1) * HALF, :] = total

    locals_["g"].wait()
    for i, k in enumerate(PEERS):
        xx, cc = column(k)
        pack(gv, gp, xx * NC + cc)
        token_copy(0, i).start()
    locals_["w"].wait()
    base_block(2)
    base_copy(2).start()
    forward(0, 1)
    base_block(1)
    base_copy(1).start()
    base_block(3)
    base_copy(3).start()
    pack(gv, gp, p)
    tokg[:, pl.ds(p, 1)] = gp[pl.ds(p, 1)].reshape(NZ, 1, CAP, -1)
    forward(0, 2)
    locals_["x"].wait()
    for i, k in enumerate(PEERS):
        xx, cc = column(k)
        pack(xv, xp, xx * NC + cc)
    pack(xv, xp, p)
    tokx[:, pl.ds(p, 1)] = xp[pl.ds(p, 1)].reshape(NZ, 1, CAP, -1)
    forward(0, 3)
    for d, f in halves(1):
        ag_copy(1, d, 1, f).start()
    for i in range(len(PEERS)):
        token_copy(1, i).start()
    for i in range(len(PEERS)):
        meta_copy(i).wait_recv()
    for zt in range(NZ):
        masks[zt] = jnp.broadcast_to(meta_r[:, zt : zt + 1, :], (PLANE, CAP, ROWS)).reshape(ROWS, ROWS)
    base_block(0)
    forward(0, HOPS)
    locals_["b"].wait()
    for i in range(len(PEERS)):
        token_copy(0, i).wait_recv()
    project(0, tokg, agb)
    forward(1, 1)
    spread(0)
    locals_["a"].wait()
    lora(z)
    lora(zplus(1))
    lora(zplus(-1))
    forward(1, 2)
    lora(zplus(2))
    lora(zplus(-2))
    forward(1, 3)
    lora(zplus(3))
    lora(zplus(-3))
    forward(1, HOPS)
    lora(zplus(HOPS))
    for i in range(len(PEERS)):
        lora_copy(i).start()
    lora_r[pl.ds(p, 1)] = lora_s[:, pl.ds(p, 1)].reshape(1, NZ, CAP, -1)
    for i in range(len(PEERS)):
        token_copy(1, i).wait_recv()
    rs_init(0)
    project(1, tokx, aga)
    rs_step(0, 1)
    spread(1)
    rs_step(0, 2)
    rs_step(0, 3)
    rs_init(1)
    rs_last(0)
    rs_step(1, 1)
    for dy in range(1, NY):
        base_copy(dy).wait_recv()
    for i in range(len(PEERS)):
        lora_copy(i).wait_recv()
    rs_step(1, 2)

    def finish(n, carry):
        rows = pl.ds(pl.multiple_of(n * ROWS, ROWS), ROWS)
        hot = jnp.where(iota((ROWS, PLANE * ROWS), 1) == idx_col[rows, :], 1.0, 0.0).astype(BF16)
        total = mm(hot, lora_r[...].reshape(PLANE * ROWS, -1)) + base_s[0, rows, :].astype(F32)
        for dy in range(1, NY):
            total = total + base_r[dy - 1, rows, :].astype(F32)
        dx_ref[rows, :] = total.astype(BF16)
        return carry

    lax.fori_loop(0, 2, finish, 0)
    rs_step(1, 3)
    lax.fori_loop(2, toks // ROWS, finish, 0)
    rs_last(1)

    for i in range(len(PEERS)):
        meta_copy(i).wait_send()
        token_copy(0, i).wait_send()
        token_copy(1, i).wait_send()
        lora_copy(i).wait_send()
    for u in (0, 1):
        for h in range(1, HOPS + 1):
            for d, f in halves(h):
                ag_copy(u, d, h, f).wait_send()
            for f in (0, 1):
                for d in (0, 1):
                    if h > 1 or f == d:
                        rs_copy(u, d, h, f).wait_send()
        for dy in range(1, NY):
            low_copy(u, dy).wait_send()
    for dy in range(1, NY):
        base_copy(dy).wait_send()


def _xzc(xc, z):
    return xc[0], z, xc[1]


def on_device(
    activations,
    output_gradient,
    frozen_weight,
    adapter_down_weight,
    adapter_up_weight,
    adapter_slot_table,
    group_adapter_index,
    group_token_length,
):
    toks, feats = activations.shape
    own = adapter_down_weight.shape[0]
    any_spec = pl.BlockSpec(memory_space=pl.ANY)
    vmem_spec = pl.BlockSpec(memory_space=pltpu.VMEM)
    dma = pltpu.SemaphoreType.DMA
    n = len(PEERS)
    return pl.pallas_call(
        kernel,
        out_shape=(
            jax.ShapeDtypeStruct((toks, feats), BF16),
            jax.ShapeDtypeStruct((own, feats), F32),
            jax.ShapeDtypeStruct((own, feats), F32),
        ),
        in_specs=[any_spec] * 5 + [vmem_spec] * 3,
        out_specs=(vmem_spec,) * 3,
        scratch_shapes=[
            pltpu.VMEM((toks, feats), BF16),
            pltpu.VMEM((toks, feats), BF16),
            pltpu.VMEM(frozen_weight.shape, BF16),
            pltpu.VMEM((PLANE, NZ, CAP, feats), BF16),
            pltpu.VMEM((PLANE, NZ, CAP, feats), BF16),
            pltpu.VMEM((NZ, PLANE, CAP, feats), BF16),
            pltpu.VMEM((NZ, PLANE, CAP, feats), BF16),
            pltpu.VMEM((NZ, ROWS, feats), BF16),
            pltpu.VMEM((NZ, ROWS, feats), BF16),
            pltpu.VMEM((PLANE, NZ, ROWS), F32),
            pltpu.VMEM((PLANE, NZ, ROWS), F32),
            pltpu.VMEM((NZ, ROWS, ROWS), F32),
            pltpu.VMEM((2, ROWS, ROWS), BF16),
            pltpu.VMEM((2, NY - 1, ROWS, ROWS), BF16),
            pltpu.VMEM((NZ, ROWS, ROWS), BF16),
            pltpu.VMEM((2, NZ, ROWS, ROWS), BF16),
            pltpu.VMEM((NY, toks, feats), BF16),
            pltpu.VMEM((NY - 1, toks, feats), BF16),
            pltpu.VMEM((NZ, PLANE, CAP, feats), BF16),
            pltpu.VMEM((PLANE, NZ, CAP, feats), BF16),
            pltpu.VMEM((2, 2, HOPS, 2, HALF, feats), BF16),
            pltpu.VMEM((2, 2, HOPS, 2, HALF, feats), BF16),
            pltpu.VMEM((1, toks), jnp.int32),
            pltpu.VMEM((toks, 1), jnp.int32),
            dma((5,)),
            dma((4, n)),
            dma((4, n)),
            dma((2, 2, HOPS, 2)),
            dma((2, 2, HOPS, 2)),
            dma((2, 2, HOPS, 2)),
            dma((2, 2, HOPS, 2)),
            dma((2, NY - 1)),
            dma((2, NY - 1)),
            dma((NY - 1,)),
            dma((NY - 1,)),
        ],
        compiler_params=pltpu.CompilerParams(
            collective_id=0, has_side_effects=True, vmem_limit_bytes=60 * 1024 * 1024
        ),
        name="lora_backward",
    )(
        activations,
        output_gradient,
        frozen_weight,
        adapter_down_weight,
        adapter_up_weight,
        adapter_slot_table.reshape(1, -1),
        group_adapter_index,
        group_token_length,
    )


def solution(mesh):
    in_specs = (
        P("adapter", "tensor"),
        P("adapter", "tensor"),
        P(None, "tensor"),
        P("adapter", "tensor"),
        P("adapter", "tensor"),
        P(),
        P("adapter", None),
        P("adapter", None),
    )
    out_specs = (P("adapter", "tensor"), P("adapter", "tensor"), P("adapter", "tensor"))
    return jax.shard_map(
        on_device, mesh=mesh, in_specs=in_specs, out_specs=out_specs, check_vma=False
    )
```

time: 332 us -> 132 us (0.40); the launches traced: 327 us -> 132 us
  waiting for transfers between devices: 183 us -> 0 us
  Pallas kernels: 0 us -> 125 us
  blocking collectives: 61.1 us -> 0 us
  matrix products: 35 us -> 0 us
  starting transfers between devices: 25.4 us -> 0 us
  between operations: 14.2 us -> 0.64 us
  other arithmetic: 4.68 us -> 0 us
    all_to_all x4 -> x0, waiting for transfers between devices: 183 us -> none  [the longest x1 49.7 us: on_device(): lax.all_to_all(partial_down.astype(jnp.bfloat16), 'adapter', split_axis=0...]
    pallas_call x0 -> x1, Pallas kernels: none -> 125 us  [on_device(): pl.pallas_call(kernel, out_shape=(jax.ShapeDtypeStruct((toks, feats), BF1...]
    all_gather x1 -> x0, blocking collectives: 46.8 us -> none  [on_device(): lax.all_gather(jnp.stack([group_slot, lengths])[None], 'adapter', axis=0,...]
    dot_general x10 -> x0, matrix products: 35 us -> none  [the longest x1 9.56 us: on_device(): lax.dot_general(frozen_weight, output_gradient, (((1,), (1,)), ((), ())),...]
    all_to_all x4 -> x0, starting transfers between devices: 25.2 us -> none  [the longest x1 6.88 us: on_device(): lax.all_to_all(outgoing_down, 'adapter', split_axis=0, concat_axis=0, til...]
    psum x1 -> x0, blocking collectives: 14.3 us -> none  [rank_sums(): lax.psum(up_part.astype(jnp.bfloat16), 'tensor').astype(jnp.float32)]
    unnamed x15 -> x3, local copies, waits for them, and re-layouts: 2.29 us -> 6.03 us
  transfers between devices with their start and end apart: 5 -> 0, of which waited for: 4 -> 0; matrix products, arithmetic and copies ran while one was open for 7% -> 0% of each run, Pallas kernels for 0% -> 0%
where the time goes in v1:
time: 132 us
  Pallas kernels  125 us (95%)
  local copies, waits for them, and re-layouts  6.03 us (5%)
    pallas_call x1, Pallas kernels, on_device(): pl.pallas_call(kernel, out_shape=(jax.ShapeDtypeStruct((toks, feats), BF1...  125 us
    unnamed x3, local copies, waits for them, and re-layouts  6.03 us

profile of v1, /device:TPU:8, one launch (start us, length us, event | category | flops | bytes accessed | tf_op | source)
XLA Modules:
  0.0 131.7 jit_solution(13777410827256141771)
XLA Ops:
  0.6 125.0 %lora_backward.1 = (bf16[512,1024]{1,0:T(8,128)(2,1)}, f32[128,1024]{1,0:T(8,128)}, f32[128,1024]{1,0:T(8,128)}) custom-call(bf16[512,1024]{1,0:T(8,128)(2,1)} %x_hbm.1, bf16[512,1024]{1,0:T(8,128)(2,1)} %g_hbm.1, bf16[4096,1024]{1,0:T(8,128)(2,1)} %w_hbm.1, bf16[128,1024]{1,0:T(8,128)(2,1)} %ad_hbm.1, bf16[128,1024]{1,0:T(8,128)(2,1)} %bu_hbm.1, ...), custom_call_target="tpu_custom_call" | custom-call | tf_op jit(solution)/shard_map/lora_backward/pallas_call | solution.py:406
  125.6 2.3 %copy.14 = bf16[512,1024]{1,0:T(8,128)(2,1)} copy(bf16[512,1024]{1,0:T(8,128)(2,1)} %get-tuple-element.6) | data formatting | bytes 2097152
  127.9 1.9 %copy.15 = f32[128,1024]{1,0:T(8,128)} copy(f32[128,1024]{1,0:T(8,128)} %get-tuple-element.7) | data formatting | bytes 1048576
  129.8 1.9 %copy.16 = f32[128,1024]{1,0:T(8,128)} copy(f32[128,1024]{1,0:T(8,128)} %get-tuple-element.8) | data formatting | bytes 1048576

commit v2 on v1

--- a/solution.py
+++ b/solution.py
@@ -19,6 +19,8 @@
 HALF = ROWS // 2
 PEERS = ((2, 0), (2, 1), (1, 0), (1, 1), (3, 0), (3, 1), (0, 1))
 DIRS = (1, NZ - 1)
+FIRST, SECOND = ((0, 0), (1, 1)), ((0, 1), (1, 0))
+NEAR = NZ // 2
 HOPS = NZ // 2
 
 NT = (((1,), (1,)), ((), ()))
@@ -37,9 +39,10 @@
     x_hbm, g_hbm, w_hbm, ad_hbm, bu_hbm, table_ref, gai_ref, len_ref,
     dx_ref, dgrad_ref, ugrad_ref,
     xv, gv, wv, xp, gp, tokx, tokg, aga, agb, meta_s, meta_r, masks,
-    low_s, low_r, wide, wide_t, base_s, base_r, lora_s, lora_r, rs_s, rs_r, idx_row, idx_col,
+    low_acc, low_s, low_r, wide, wide_t, base_s, base_r, lora_s, lora_r, rs_s, rs_r, idx_row, idx_col,
     local_sem, x_send, x_recv, ag_send, ag_recv, rs_send, rs_recv, low_send, low_recv, base_send, base_recv,
 ):
+    toks = gv.shape[0]
     me = lax.axis_index("adapter")
     y = lax.axis_index("tensor")
     x = lax.div(me, NZ * NC)
@@ -57,9 +60,8 @@
         dx, dc = k
         return lax.rem(x + dx, NX), lax.rem(c + dc, NC)
 
-    def column_from(k):
-        dx, dc = k
-        return lax.rem(x + (NX - dx), NX), lax.rem(c + dc, NC)
+    def owner_z_of(e):
+        return zplus(e + 2)
 
     locals_ = {
         "g": pltpu.make_async_copy(g_hbm, gv, local_sem.at[0]),
@@ -77,17 +79,18 @@
         )
 
     def token_copy(unit, i):
-        packed, landed = ((gp, tokg), (xp, tokx))[unit]
-        xx, cc = column(PEERS[i])
-        return plane_copy(unit, i, packed.at[xx * NC + cc], landed.at[:, p])
+        packed, landed, first, count = ((gp, tokg, 0, NZ), (xp, tokx, 0, NEAR), (xp, tokx, NEAR, NZ - NEAR))[unit]
+        xx, cc = column(PEERS[i])
+        entries = pl.ds(first, count)
+        return plane_copy(unit, i, packed.at[xx * NC + cc, entries], landed.at[entries, p])
 
     def meta_copy(i):
         xx, cc = column(PEERS[i])
-        return plane_copy(3, i, meta_s.at[xx * NC + cc], meta_r.at[p])
+        return plane_copy(4, i, meta_s.at[xx * NC + cc], meta_r.at[p])
 
     def lora_copy(i):
         xx, cc = column(PEERS[i])
-        return plane_copy(2, i, lora_s.at[:, xx * NC + cc], lora_r.at[p])
+        return plane_copy(3, i, lora_s.at[:, xx * NC + cc], lora_r.at[p])
 
     def ag_copy(u, d, h, f):
         own = (bu_hbm, ad_hbm)[u]
@@ -115,15 +118,16 @@
             device_id=(me, lax.rem(y + dy, NY)), device_id_type=MESH,
         )
 
-    def base_copy(dy):
+    def base_copy(dy, f):
+        rows = pl.ds(f * (toks // 2), toks // 2)
         return pltpu.make_async_remote_copy(
-            src_ref=base_s.at[dy], dst_ref=base_r.at[dy - 1],
-            send_sem=base_send.at[dy - 1], recv_sem=base_recv.at[dy - 1],
+            src_ref=base_s.at[dy, rows], dst_ref=base_r.at[dy - 1, rows],
+            send_sem=base_send.at[dy - 1, f], recv_sem=base_recv.at[dy - 1, f],
             device_id=(me, lax.rem(y + dy, NY)), device_id_type=MESH,
         )
 
     def halves(h):
-        return [(d, f) for f in (0, 1) for d in (0, 1) if h < HOPS or f == d]
+        return FIRST + SECOND if h < HOPS else FIRST
 
     for name in ("g", "b", "x", "w", "a"):
         locals_[name].start()
@@ -135,7 +139,6 @@
         pl.semaphore_signal(barrier, inc=1, device_id=partner, device_id_type=MESH)
 
     ng = gai_ref.shape[1]
-    toks = gv.shape[0]
     eye = iota((ng, ng), 0) == iota((ng, ng), 1)
 
     def to_col(row):
@@ -155,7 +158,7 @@
     owner_c = (slot >> 3) & 1
     owner_z = (slot >> 4) & (NZ - 1)
     owner_x = slot >> 7
-    pair = (owner_x * NC + owner_c) * NZ + owner_z
+    pair = (owner_x * NC + owner_c) * NZ + ((owner_z + (NZ - 2) + (NZ - z)) & (NZ - 1))
     start = jnp.sum(jnp.where(iota((ng, ng), 1) < iota((ng, ng), 0), len_row, 0.0), axis=1, keepdims=True)
     shift = (pair * CAP).astype(F32) - start
     end = start + len_col
@@ -187,8 +190,8 @@
         hot = jnp.where(iota((ROWS, toks), 0) + q * ROWS == idx_row[...], 1.0, 0.0).astype(BF16)
         packed[q] = mm(hot, source[...]).astype(BF16).reshape(NZ, CAP, -1)
 
-    def forward(u, h):
-        for d, f in halves(h):
+    def forward(u, h, part):
+        for d, f in part:
             source = zplus(-h if d == 0 else h)
             buf = (agb, aga)[u]
             landed = buf.at[source, pl.ds(f * HALF, HALF)]
@@ -211,18 +214,26 @@
 
         lax.fori_loop(0, wv.shape[1] // width, tile, 0)
 
-    def select(zt, transposed):
+    def select(e, transposed):
         a, b = iota((ROWS, ROWS), 0), iota((ROWS, ROWS), 1)
         narrow, broad = (a, b) if transposed else (b, a)
-        return jnp.where(narrow == zt * RANK + (broad & (RANK - 1)), 1.0, 0.0).astype(BF16)
-
-    def project(u, tok, weights):
-        def block(zt, acc):
-            wide_p = mm(tok[zt].reshape(ROWS, -1), weights[zt], NT) * masks[zt]
-            return acc + mm(wide_p.astype(BF16), select(zt, False))
-
-        acc = lax.fori_loop(0, NZ, block, jnp.zeros((ROWS, ROWS), F32))
-        low_s[u] = acc.astype(BF16)
+        return jnp.where(narrow == e * RANK + (broad & (RANK - 1)), 1.0, 0.0).astype(BF16)
+
+    toks_of = (tokx, tokg)
+    project_of = (tokg, tokx)
+    maps_of = (agb, aga)
+
+    def project(u, first, count):
+        def block(e, carry):
+            wide_p = mm(project_of[u][e].reshape(ROWS, -1), maps_of[u][owner_z_of(e)], NT) * masks[e]
+            part_low = mm(wide_p.astype(BF16), select(e, False))
+            low_acc[...] = jnp.where(e == 0, part_low, low_acc[...] + part_low)
+            return carry
+
+        lax.fori_loop(first, first + count, block, 0)
+
+    def low_sends(u):
+        low_s[u] = low_acc[...].astype(BF16)
         for dy in (2, 1, 3):
             low_copy(u, dy).start()
 
@@ -233,122 +244,48 @@
             total = total + low_r[u, dy - 1].astype(F32)
         low = total.astype(BF16)
 
-        def block(zt, carry):
-            twice = mm(low, select(zt, True)) * (2.0 * masks[zt])
+        def block(e, carry):
+            twice = mm(low, select(e, True)) * (2.0 * masks[e])
             if u == 0:
-                wide[zt] = twice.astype(BF16)
-            wide_t[u, zt] = twice.T.astype(BF16)
+                wide[e] = twice.astype(BF16)
+            wide_t[u, e] = twice.T.astype(BF16)
             return carry
 
         lax.fori_loop(0, NZ, block, 0)
 
-    def lora(zt):
-        lora_s[zt] = mm(wide[zt], aga[zt]).astype(BF16).reshape(PLANE, CAP, -1)
-
-    toks_of = (tokx, tokg)
-
-    def term(u, zt, f):
-        return mm(wide_t[u, zt, f * HALF : (f + 1) * HALF, :], toks_of[u][zt].reshape(ROWS, -1))
+    def lora(distance):
+        e = (distance - 2) % NZ
+        lora_s[e] = mm(wide[e], aga[zplus(distance)]).astype(BF16).reshape(PLANE, CAP, -1)
+
+    def term(u, distance, f):
+        e = (distance - 2) % NZ
+        return mm(wide_t[u, e, f * HALF : (f + 1) * HALF, :], toks_of[u][e].reshape(ROWS, -1))
 
     def rs_target(d, h):
-        return zplus((HOPS + 1 - h) if d == 0 else -(HOPS + 1 - h))
+        return (HOPS + 1 - h) if d == 0 else -(HOPS + 1 - h)
 
     def rs_init(u):
-        for h in (1, 2):
-            for d in (0, 1):
-                f = d if h == 1 else 1 - d
+        for h, part in ((1, FIRST), (2, SECOND)):
+            for d, f in part:
                 rs_s[u, d, h - 1, f] = term(u, rs_target(d, h), f).astype(BF16)
                 rs_copy(u, d, h, f).start()
 
-    def rs_step(u, h):
-        for f in (0, 1):
-            for d in (0, 1):
-                if h == 1 and f != d:
-                    continue
-                rs_copy(u, d, h, f).wait_recv()
-                total = rs_r[u, d, h - 1, f].astype(F32) + term(u, rs_target(d, h + 1), f)
-                rs_s[u, d, h, f] = total.astype(BF16)
-                rs_copy(u, d, h + 1, f).start()
+    def rs_step(u, h, part):
+        for d, f in part:
+            rs_copy(u, d, h, f).wait_recv()
+            total = rs_r[u, d, h - 1, f].astype(F32) + term(u, rs_target(d, h + 1), f)
+            rs_s[u, d, h, f] = total.astype(BF16)
+            rs_copy(u, d, h + 1, f).start()
 
     def rs_last(u):
         out = (dgrad_ref, ugrad_ref)[u]
-        for f in (0, 1):
-            total = term(u, z, f)
-            for d in (0, 1):
-                rs_copy(u, d, HOPS, f).wait_recv()
-                total = total + rs_r[u, d, HOPS - 1, f].astype(F32)
-            out[f * HALF : (f + 1) * HALF, :] = total
-
-    locals_["g"].wait()
-    for i, k in enumerate(PEERS):
-        xx, cc = column(k)
-        pack(gv, gp, xx * NC + cc)
-        token_copy(0, i).start()
-    locals_["w"].wait()
-    base_block(2)
-    base_copy(2).start()
-    forward(0, 1)
-    base_block(1)
-    base_copy(1).start()
-    base_block(3)
-    base_copy(3).start()
-    pack(gv, gp, p)
-    tokg[:, pl.ds(p, 1)] = gp[pl.ds(p, 1)].reshape(NZ, 1, CAP, -1)
-    forward(0, 2)
-    locals_["x"].wait()
-    for i, k in enumerate(PEERS):
-        xx, cc = column(k)
-        pack(xv, xp, xx * NC + cc)
-    pack(xv, xp, p)
-    tokx[:, pl.ds(p, 1)] = xp[pl.ds(p, 1)].reshape(NZ, 1, CAP, -1)
-    forward(0, 3)
-    for d, f in halves(1):
-        ag_copy(1, d, 1, f).start()
-    for i in range(len(PEERS)):
-        token_copy(1, i).start()
-    for i in range(len(PEERS)):
-        meta_copy(i).wait_recv()
-    for zt in range(NZ):
-        masks[zt] = jnp.broadcast_to(meta_r[:, zt : zt + 1, :], (PLANE, CAP, ROWS)).reshape(ROWS, ROWS)
-    base_block(0)
-    forward(0, HOPS)
-    locals_["b"].wait()
-    for i in range(len(PEERS)):
-        token_copy(0, i).wait_recv()
-    project(0, tokg, agb)
-    forward(1, 1)
-    spread(0)
-    locals_["a"].wait()
-    lora(z)
-    lora(zplus(1))
-    lora(zplus(-1))
-    forward(1, 2)
-    lora(zplus(2))
-    lora(zplus(-2))
-    forward(1, 3)
-    lora(zplus(3))
-    lora(zplus(-3))
-    forward(1, HOPS)
-    lora(zplus(HOPS))
-    for i in range(len(PEERS)):
-        lora_copy(i).start()
-    lora_r[pl.ds(p, 1)] = lora_s[:, pl.ds(p, 1)].reshape(1, NZ, CAP, -1)
-    for i in range(len(PEERS)):
-        token_copy(1, i).wait_recv()
-    rs_init(0)
-    project(1, tokx, aga)
-    rs_step(0, 1)
-    spread(1)
-    rs_step(0, 2)
-    rs_step(0, 3)
-    rs_init(1)
-    rs_last(0)
-    rs_step(1, 1)
-    for dy in range(1, NY):
-        base_copy(dy).wait_recv()
-    for i in range(len(PEERS)):
-        lora_copy(i).wait_recv()
-    rs_step(1, 2)
+        own = [term(u, 0, f) for f in (0, 1)]
+        for d, f in SECOND:
+            rs_copy(u, d, HOPS, f).wait_recv()
+            own[f] = own[f] + rs_r[u, d, HOPS - 1, f].astype(F32)
+        for d, f in FIRST:
+            rs_copy(u, d, HOPS, f).wait_recv()
+            out[f * HALF : (f + 1) * HALF, :] = own[f] + rs_r[u, d, HOPS - 1, f].astype(F32)
 
     def finish(n, carry):
         rows = pl.ds(pl.multiple_of(n * ROWS, ROWS), ROWS)
@@ -359,15 +296,113 @@
         dx_ref[rows, :] = total.astype(BF16)
         return carry
 
+    def own_tokens(packed, landed):
+        pack(gv if packed is gp else xv, packed, p)
+        landed[:, pl.ds(p, 1)] = packed[pl.ds(p, 1)].reshape(NZ, 1, CAP, -1)
+
+    every = range(len(PEERS))
+    locals_["g"].wait()
+    for i in every:
+        xx, cc = column(PEERS[i])
+        pack(gv, gp, xx * NC + cc)
+        token_copy(0, i).start()
+    forward(0, 1, FIRST)
+    locals_["w"].wait()
+    base_block(1)
+    for f in (0, 1):
+        base_copy(1, f).start()
+    forward(0, 1, SECOND)
+    base_block(3)
+    for f in (0, 1):
+        base_copy(3, f).start()
+    forward(0, 2, FIRST)
+    locals_["x"].wait()
+    for i in every[:4]:
+        xx, cc = column(PEERS[i])
+        pack(xv, xp, xx * NC + cc)
+        token_copy(1, i).start()
+    forward(0, 2, SECOND)
+    for i in every[4:]:
+        xx, cc = column(PEERS[i])
+        pack(xv, xp, xx * NC + cc)
+        token_copy(1, i).start()
+    for i in every:
+        token_copy(2, i).start()
+    forward(0, 3, FIRST)
+    for d, f in FIRST:
+        ag_copy(1, d, 1, f).start()
+    own_tokens(gp, tokg)
+    forward(0, 3, SECOND)
+    for d, f in SECOND:
+        ag_copy(1, d, 1, f).start()
+    own_tokens(xp, tokx)
+    for i in every:
+        meta_copy(i).wait_recv()
+    for e in range(NZ):
+        masks[e] = jnp.broadcast_to(meta_r[:, e : e + 1, :], (PLANE, CAP, ROWS)).reshape(ROWS, ROWS)
+    base_block(2)
+    forward(0, HOPS, FIRST)
+    locals_["b"].wait()
+    forward(1, 1, FIRST)
+    for i in every:
+        token_copy(0, i).wait_recv()
+    project(0, 0, NZ // 2)
+    forward(1, 1, SECOND)
+    project(0, NZ // 2, NZ // 2)
+    low_sends(0)
+    base_copy(2, 0).start()
+    forward(1, 2, FIRST)
+    spread(0)
+    forward(1, 2, SECOND)
+    locals_["a"].wait()
+    for distance in (0, 1, -1, 2, -2):
+        lora(distance)
+    forward(1, 3, FIRST)
+    for i in every:
+        token_copy(1, i).wait_recv()
+    forward(1, 3, SECOND)
+    rs_init(0)
+    lora(3)
+    lora(-3)
+    forward(1, HOPS, FIRST)
+    lora(HOPS)
+    for i in every:
+        lora_copy(i).start()
+    lora_r[pl.ds(p, 1)] = lora_s[:, pl.ds(p, 1)].reshape(1, NZ, CAP, -1)
+    project(1, 0, NEAR)
+    rs_step(0, 1, FIRST)
+    for i in every:
+        token_copy(2, i).wait_recv()
+    rs_step(0, 2, SECOND)
+    project(1, NEAR, NZ - NEAR)
+    low_sends(1)
+    base_copy(2, 1).start()
+    rs_step(0, 2, FIRST)
+    base_block(0)
+    rs_step(0, 3, SECOND)
+    spread(1)
+    rs_step(0, 3, FIRST)
+    rs_init(1)
+    rs_last(0)
+    rs_step(1, 1, FIRST)
+    rs_step(1, 2, SECOND)
+    rs_step(1, 2, FIRST)
+    for i in every:
+        lora_copy(i).wait_recv()
+    for f in (0, 1):
+        for dy in range(1, NY):
+            base_copy(dy, f).wait_recv()
     lax.fori_loop(0, 2, finish, 0)
-    rs_step(1, 3)
-    lax.fori_loop(2, toks // ROWS, finish, 0)
+    rs_step(1, 3, SECOND)
+    lax.fori_loop(2, 3, finish, 0)
+    rs_step(1, 3, FIRST)
+    lax.fori_loop(3, toks // ROWS, finish, 0)
     rs_last(1)
 
     for i in range(len(PEERS)):
         meta_copy(i).wait_send()
-        token_copy(0, i).wait_send()
-        token_copy(1, i).wait_send()
+        for unit in range(3):
+            token_copy(unit, i).wait_send()
         lora_copy(i).wait_send()
     for u in (0, 1):
         for h in range(1, HOPS + 1):
@@ -380,11 +415,20 @@
         for dy in range(1, NY):
             low_copy(u, dy).wait_send()
     for dy in range(1, NY):
-        base_copy(dy).wait_send()
+        for f in (0, 1):
+            base_copy(dy, f).wait_send()
 
 
 def _xzc(xc, z):
     return xc[0], z, xc[1]
+
+
+def emit(*refs):
+    copies = [pltpu.make_async_copy(refs[i], refs[3 + i], refs[6].at[i]) for i in range(3)]
+    for copy in copies:
+        copy.start()
+    for copy in copies:
+        copy.wait()
 
 
 def on_device(
@@ -403,7 +447,7 @@
     vmem_spec = pl.BlockSpec(memory_space=pltpu.VMEM)
     dma = pltpu.SemaphoreType.DMA
     n = len(PEERS)
-    return pl.pallas_call(
+    results = pl.pallas_call(
         kernel,
         out_shape=(
             jax.ShapeDtypeStruct((toks, feats), BF16),
@@ -425,6 +469,7 @@
             pltpu.VMEM((PLANE, NZ, ROWS), F32),
             pltpu.VMEM((PLANE, NZ, ROWS), F32),
             pltpu.VMEM((NZ, ROWS, ROWS), F32),
+            pltpu.VMEM((ROWS, ROWS), F32),
             pltpu.VMEM((2, ROWS, ROWS), BF16),
             pltpu.VMEM((2, NY - 1, ROWS, ROWS), BF16),
             pltpu.VMEM((NZ, ROWS, ROWS), BF16),
@@ -438,16 +483,16 @@
             pltpu.VMEM((1, toks), jnp.int32),
             pltpu.VMEM((toks, 1), jnp.int32),
             dma((5,)),
-            dma((4, n)),
-            dma((4, n)),
+            dma((5, n)),
+            dma((5, n)),
             dma((2, 2, HOPS, 2)),
             dma((2, 2, HOPS, 2)),
             dma((2, 2, HOPS, 2)),
             dma((2, 2, HOPS, 2)),
             dma((2, NY - 1)),
             dma((2, NY - 1)),
-            dma((NY - 1,)),
-            dma((NY - 1,)),
+            dma((NY - 1, 2)),
+            dma((NY - 1, 2)),
         ],
         compiler_params=pltpu.CompilerParams(
             collective_id=0, has_side_effects=True, vmem_limit_bytes=60 * 1024 * 1024
@@ -463,6 +508,14 @@
         group_adapter_index,
         group_token_length,
     )
+    return pl.pallas_call(
+        emit,
+        out_shape=tuple(jax.ShapeDtypeStruct(r.shape, r.dtype) for r in results),
+        in_specs=[any_spec] * 3,
+        out_specs=(any_spec,) * 3,
+        scratch_shapes=[dma((3,))],
+        name="emit",
+    )(*results)
 
 
 def solution(mesh):

time: 132 us -> 168 us (1.27)
  Pallas kernels: 125 us -> 166 us
  local copies, waits for them, and re-layouts: 6.03 us -> 0 us
    pallas_call x0 -> x1, Pallas kernels: none -> 64.7 us  [on_device(): pl.pallas_call(emit, out_shape=tuple((jax.ShapeDtypeStruct(r.shape, r.dty...]
    pallas_call x1, Pallas kernels: 125 us -> 101 us  [on_device(): pl.pallas_call(kernel, out_shape=(jax.ShapeDtypeStruct((toks, feats), BF1...]
    unnamed x3 -> x0, local copies, waits for them, and re-layouts: 6.03 us -> none
where the time goes in v2:
time: 168 us; the launch traced here: 167 us
  Pallas kernels  166 us (99%)
    pallas_call x1, Pallas kernels, on_device(): pl.pallas_call(kernel, out_shape=(jax.ShapeDtypeStruct((toks, feats), BF1...  101 us
    pallas_call x1, Pallas kernels, on_device(): pl.pallas_call(emit, out_shape=tuple((jax.ShapeDtypeStruct(r.shape, r.dty...  64.7 us

profile of v2, /device:TPU:8, one launch (start us, length us, event | category | flops | bytes accessed | tf_op | source)
XLA Modules:
  0.0 166.5 jit_solution(1430997505106897795)
XLA Ops:
  0.6 101.2 %lora_backward.1 = (bf16[512,1024]{1,0:T(8,128)(2,1)}, f32[128,1024]{1,0:T(8,128)}, f32[128,1024]{1,0:T(8,128)}) custom-call(bf16[512,1024]{1,0:T(8,128)(2,1)} %x_hbm.1, bf16[512,1024]{1,0:T(8,128)(2,1)} %g_hbm.1, bf16[4096,1024]{1,0:T(8,128)(2,1)} %w_hbm.1, bf16[128,1024]{1,0:T(8,128)(2,1)} %ad_hbm.1, bf16[128,1024]{1,0:T(8,128)(2,1)} %bu_hbm.1, ...), custom_call_target="tpu_custom_call" | custom-call | tf_op jit(solution)/shard_map/lora_backward/pallas_call | solution.py:450
  101.9 64.7 %emit.1 = (bf16[512,1024]{1,0:T(8,128)(2,1)}, f32[128,1024]{1,0:T(8,128)}, f32[128,1024]{1,0:T(8,128)}) custom-call(bf16[512,1024]{1,0:T(8,128)(2,1)} %get-tuple-element.6.refs_0_, f32[128,1024]{1,0:T(8,128)} %get-tuple-element.7.refs_1_, f32[128,1024]{1,0:T(8,128)} %get-tuple-element.8.refs_2_), custom_call_target="tpu_custom_call" | custom-call | tf_op jit(solution)/shard_map/emit/pallas_call | solution.py:511

commit v3 on v2

--- a/solution.py
+++ b/solution.py
@@ -450,9 +450,9 @@
     results = pl.pallas_call(
         kernel,
         out_shape=(
-            jax.ShapeDtypeStruct((toks, feats), BF16),
-            jax.ShapeDtypeStruct((own, feats), F32),
-            jax.ShapeDtypeStruct((own, feats), F32),
+            pltpu.VMEM((toks, feats), BF16),
+            pltpu.VMEM((own, feats), F32),
+            pltpu.VMEM((own, feats), F32),
         ),
         in_specs=[any_spec] * 5 + [vmem_spec] * 3,
         out_specs=(vmem_spec,) * 3,
@@ -511,11 +511,11 @@
     return pl.pallas_call(
         emit,
         out_shape=tuple(jax.ShapeDtypeStruct(r.shape, r.dtype) for r in results),
-        in_specs=[any_spec] * 3,
+        in_specs=[vmem_spec] * 3,
         out_specs=(any_spec,) * 3,
         scratch_shapes=[dma((3,))],
         name="emit",
-    )(*results)
+    )(*(pltpu.with_memory_space_constraint(r, pltpu.VMEM) for r in results))
 
 
 def solution(mesh):

time: 168 us -> 103 us (0.61)
  Pallas kernels: 166 us -> 101 us
    pallas_call x1, Pallas kernels: 64.7 us -> 1.34 us  [on_device(): pl.pallas_call(emit, out_shape=tuple((jax.ShapeDtypeStruct(r.shape, r.dty...]
where the time goes in v3:
time: 103 us; the launch traced here: 102 us
  Pallas kernels  101 us (98%)
    pallas_call x1, Pallas kernels, on_device(): pl.pallas_call(kernel, out_shape=(pltpu.VMEM((toks, feats), BF16), pltpu....  99.9 us

profile of v3, /device:TPU:8, one launch (start us, length us, event | category | flops | bytes accessed | tf_op | source)
XLA Modules:
  0.0 101.9 jit_solution(9132802598501830203)
XLA Ops:
  0.6 99.9 %lora_backward.1 = (bf16[512,1024]{1,0:T(8,128)(2,1)S(1)}, f32[128,1024]{1,0:T(8,128)S(1)}, f32[128,1024]{1,0:T(8,128)S(1)}) custom-call(bf16[512,1024]{1,0:T(8,128)(2,1)} %x_hbm.1, bf16[512,1024]{1,0:T(8,128)(2,1)} %g_hbm.1, bf16[4096,1024]{1,0:T(8,128)(2,1)} %w_hbm.1, bf16[128,1024]{1,0:T(8,128)(2,1)} %ad_hbm.1, bf16[128,1024]{1,0:T(8,128)(2,1)} %bu_hbm.1, ...), custom_call_target="tpu_custom_call" | custom-call | tf_op jit(solution)/shard_map/lora_backward/pallas_call | solution.py:450
  100.5 1.3 %emit.1 = (bf16[512,1024]{1,0:T(8,128)(2,1)}, f32[128,1024]{1,0:T(8,128)}, f32[128,1024]{1,0:T(8,128)}) custom-call(bf16[512,1024]{1,0:T(8,128)(2,1)S(1)} %get-tuple-element.6.refs_0_, f32[128,1024]{1,0:T(8,128)S(1)} %get-tuple-element.7.refs_1_, f32[128,1024]{1,0:T(8,128)S(1)} %get-tuple-element.8.refs_2_), custom_call_target="tpu_custom_call" | custom-call | tf_op jit(solution)/shard_map/emit/pallas_call | solution.py:511

commit v4 on v3

--- a/solution.py
+++ b/solution.py
@@ -119,11 +119,12 @@
         )
 
     def base_copy(dy, f):
+        hop = dy if dy != 2 else (1, NY - 1)[f]
         rows = pl.ds(f * (toks // 2), toks // 2)
         return pltpu.make_async_remote_copy(
             src_ref=base_s.at[dy, rows], dst_ref=base_r.at[dy - 1, rows],
             send_sem=base_send.at[dy - 1, f], recv_sem=base_recv.at[dy - 1, f],
-            device_id=(me, lax.rem(y + dy, NY)), device_id_type=MESH,
+            device_id=(me, lax.rem(y + hop, NY)), device_id_type=MESH,
         )
 
     def halves(h):
@@ -214,6 +215,12 @@
 
         lax.fori_loop(0, wv.shape[1] // width, tile, 0)
 
+    def base_relay(dy, f):
+        base_copy(2, f).wait_recv()
+        rows = pl.ds(f * (toks // 2), toks // 2)
+        base_s[dy, rows, :] = (base_s[dy, rows, :].astype(F32) + base_r[1, rows, :].astype(F32)).astype(BF16)
+        base_copy(dy, f).start()
+
     def select(e, transposed):
         a, b = iota((ROWS, ROWS), 0), iota((ROWS, ROWS), 1)
         narrow, broad = (a, b) if transposed else (b, a)
@@ -291,7 +298,7 @@
         rows = pl.ds(pl.multiple_of(n * ROWS, ROWS), ROWS)
         hot = jnp.where(iota((ROWS, PLANE * ROWS), 1) == idx_col[rows, :], 1.0, 0.0).astype(BF16)
         total = mm(hot, lora_r[...].reshape(PLANE * ROWS, -1)) + base_s[0, rows, :].astype(F32)
-        for dy in range(1, NY):
+        for dy in (1, NY - 1):
             total = total + base_r[dy - 1, rows, :].astype(F32)
         dx_ref[rows, :] = total.astype(BF16)
         return carry
@@ -308,13 +315,12 @@
         token_copy(0, i).start()
     forward(0, 1, FIRST)
     locals_["w"].wait()
+    base_block(2)
+    for f in (0, 1):
+        base_copy(2, f).start()
+    forward(0, 1, SECOND)
     base_block(1)
-    for f in (0, 1):
-        base_copy(1, f).start()
-    forward(0, 1, SECOND)
-    base_block(3)
-    for f in (0, 1):
-        base_copy(3, f).start()
+    base_copy(1, 1).start()
     forward(0, 2, FIRST)
     locals_["x"].wait()
     for i in every[:4]:
@@ -322,6 +328,8 @@
         pack(xv, xp, xx * NC + cc)
         token_copy(1, i).start()
     forward(0, 2, SECOND)
+    base_block(3)
+    base_copy(3, 0).start()
     for i in every[4:]:
         xx, cc = column(PEERS[i])
         pack(xv, xp, xx * NC + cc)
@@ -340,7 +348,6 @@
         meta_copy(i).wait_recv()
     for e in range(NZ):
         masks[e] = jnp.broadcast_to(meta_r[:, e : e + 1, :], (PLANE, CAP, ROWS)).reshape(ROWS, ROWS)
-    base_block(2)
     forward(0, HOPS, FIRST)
     locals_["b"].wait()
     forward(1, 1, FIRST)
@@ -350,7 +357,8 @@
     forward(1, 1, SECOND)
     project(0, NZ // 2, NZ // 2)
     low_sends(0)
-    base_copy(2, 0).start()
+    base_relay(1, 0)
+    base_relay(3, 1)
     forward(1, 2, FIRST)
     spread(0)
     forward(1, 2, SECOND)
@@ -376,7 +384,6 @@
     rs_step(0, 2, SECOND)
     project(1, NEAR, NZ - NEAR)
     low_sends(1)
-    base_copy(2, 1).start()
     rs_step(0, 2, FIRST)
     base_block(0)
     rs_step(0, 3, SECOND)
@@ -387,16 +394,14 @@
     rs_step(1, 1, FIRST)
     rs_step(1, 2, SECOND)
     rs_step(1, 2, FIRST)
+    rs_step(1, 3, SECOND)
+    rs_step(1, 3, FIRST)
     for i in every:
         lora_copy(i).wait_recv()
     for f in (0, 1):
-        for dy in range(1, NY):
+        for dy in (1, NY - 1):
             base_copy(dy, f).wait_recv()
-    lax.fori_loop(0, 2, finish, 0)
-    rs_step(1, 3, SECOND)
-    lax.fori_loop(2, 3, finish, 0)
-    rs_step(1, 3, FIRST)
-    lax.fori_loop(3, toks // ROWS, finish, 0)
+    lax.fori_loop(0, toks // ROWS, finish, 0)
     rs_last(1)
 
     for i in range(len(PEERS)):

time: 103 us -> 96.8 us (0.940)
  Pallas kernels: 101 us -> 95.3 us
    pallas_call x1, Pallas kernels: 99.9 us -> 94 us  [on_device(): pl.pallas_call(kernel, out_shape=(pltpu.VMEM((toks, feats), BF16), pltpu....]
where the time goes in v4:
time: 96.8 us; the launch traced here: 95.9 us
  Pallas kernels  95.3 us (98%)
    pallas_call x1, Pallas kernels, on_device(): pl.pallas_call(kernel, out_shape=(pltpu.VMEM((toks, feats), BF16), pltpu....  94 us

profile of v4, /device:TPU:8, one launch (start us, length us, event | category | flops | bytes accessed | tf_op | source)
XLA Modules:
  0.0 95.9 jit_solution(1469344225339979989)
XLA Ops:
  0.6 94.0 %lora_backward.1 = (bf16[512,1024]{1,0:T(8,128)(2,1)S(1)}, f32[128,1024]{1,0:T(8,128)S(1)}, f32[128,1024]{1,0:T(8,128)S(1)}) custom-call(bf16[512,1024]{1,0:T(8,128)(2,1)} %x_hbm.1, bf16[512,1024]{1,0:T(8,128)(2,1)} %g_hbm.1, bf16[4096,1024]{1,0:T(8,128)(2,1)} %w_hbm.1, bf16[128,1024]{1,0:T(8,128)(2,1)} %ad_hbm.1, bf16[128,1024]{1,0:T(8,128)(2,1)} %bu_hbm.1, ...), custom_call_target="tpu_custom_call" | custom-call | tf_op jit(solution)/shard_map/lora_backward/pallas_call | solution.py:455
  94.6 1.3 %emit.1 = (bf16[512,1024]{1,0:T(8,128)(2,1)}, f32[128,1024]{1,0:T(8,128)}, f32[128,1024]{1,0:T(8,128)}) custom-call(bf16[512,1024]{1,0:T(8,128)(2,1)S(1)} %get-tuple-element.6.refs_0_, f32[128,1024]{1,0:T(8,128)S(1)} %get-tuple-element.7.refs_1_, f32[128,1024]{1,0:T(8,128)S(1)} %get-tuple-element.8.refs_2_), custom_call_target="tpu_custom_call" | custom-call | tf_op jit(solution)/shard_map/emit/pallas_call | solution.py:516

commit v5 on v4

--- a/solution.py
+++ b/solution.py
@@ -20,8 +20,10 @@
 PEERS = ((2, 0), (2, 1), (1, 0), (1, 1), (3, 0), (3, 1), (0, 1))
 DIRS = (1, NZ - 1)
 FIRST, SECOND = ((0, 0), (1, 1)), ((0, 1), (1, 0))
-NEAR = NZ // 2
 HOPS = NZ // 2
+PIECES = 2
+TOKENS = ((0, 0, 3), (1, 0, 3), (0, 3, 2), (1, 3, 2), (0, 5, 3), (1, 5, 2), (1, 7, 1))
+LOWS = (((0, 3), (3, 2), (5, 3)), ((0, 5), (5, 3)))
 
 NT = (((1,), (1,)), ((), ()))
 NN = (((1,), (0,)), ((), ()))
@@ -35,11 +37,16 @@
     return lax.broadcasted_iota(jnp.int32, shape, dim)
 
 
+def entry_of(distance):
+    ahead = distance % NZ
+    return max(NZ - 1 - 2 * min(ahead, NZ - ahead) + (ahead > HOPS), 0)
+
+
 def kernel(
-    x_hbm, g_hbm, w_hbm, ad_hbm, bu_hbm, table_ref, gai_ref, len_ref,
+    x_hbm, g_hbm, w_hbm, ad_hbm, bu_hbm, table_hbm, gai_hbm, len_hbm,
     dx_ref, dgrad_ref, ugrad_ref,
     xv, gv, wv, xp, gp, tokx, tokg, aga, agb, meta_s, meta_r, masks,
-    low_acc, low_s, low_r, wide, wide_t, base_s, base_r, lora_s, lora_r, rs_s, rs_r, idx_row, idx_col,
+    low_acc, low_s, low_r, wide, wide_t, base_s, base_r, lora_s, lora_r, rs_s, rs_r, idx_row, idx_col, table_ref, gai_ref, len_ref,
     local_sem, x_send, x_recv, ag_send, ag_recv, rs_send, rs_recv, low_send, low_recv, base_send, base_recv,
 ):
     toks = gv.shape[0]
@@ -61,7 +68,8 @@
         return lax.rem(x + dx, NX), lax.rem(c + dc, NC)
 
     def owner_z_of(e):
-        return zplus(e + 2)
+        distance, odd = lax.div(NZ - e, 2), lax.rem(e, 2)
+        return zplus(odd * distance + (1 - odd) * (NZ - distance))
 
     locals_ = {
         "g": pltpu.make_async_copy(g_hbm, gv, local_sem.at[0]),
@@ -69,6 +77,9 @@
         "b": pltpu.make_async_copy(bu_hbm, agb.at[z], local_sem.at[2]),
         "a": pltpu.make_async_copy(ad_hbm, aga.at[z], local_sem.at[3]),
         "w": pltpu.make_async_copy(w_hbm, wv, local_sem.at[4]),
+        "table": pltpu.make_async_copy(table_hbm, table_ref, local_sem.at[5]),
+        "gai": pltpu.make_async_copy(gai_hbm, gai_ref, local_sem.at[6]),
+        "len": pltpu.make_async_copy(len_hbm, len_ref, local_sem.at[7]),
     }
 
     def plane_copy(unit, i, src, dst):
@@ -79,18 +90,19 @@
         )
 
     def token_copy(unit, i):
-        packed, landed, first, count = ((gp, tokg, 0, NZ), (xp, tokx, 0, NEAR), (xp, tokx, NEAR, NZ - NEAR))[unit]
+        kind, first, count = TOKENS[unit]
+        packed, landed = ((gp, tokg), (xp, tokx))[kind]
         xx, cc = column(PEERS[i])
         entries = pl.ds(first, count)
         return plane_copy(unit, i, packed.at[xx * NC + cc, entries], landed.at[entries, p])
 
     def meta_copy(i):
         xx, cc = column(PEERS[i])
-        return plane_copy(4, i, meta_s.at[xx * NC + cc], meta_r.at[p])
+        return plane_copy(len(TOKENS) + 1, i, meta_s.at[xx * NC + cc], meta_r.at[p])
 
     def lora_copy(i):
         xx, cc = column(PEERS[i])
-        return plane_copy(3, i, lora_s.at[:, xx * NC + cc], lora_r.at[p])
+        return plane_copy(len(TOKENS), i, lora_s.at[:, xx * NC + cc], lora_r.at[p])
 
     def ag_copy(u, d, h, f):
         own = (bu_hbm, ad_hbm)[u]
@@ -111,16 +123,16 @@
             device_id=(at(x, zplus(DIRS[d]), c), y), device_id_type=MESH,
         )
 
-    def low_copy(u, dy):
+    def low_copy(u, part, dy):
         return pltpu.make_async_remote_copy(
-            src_ref=low_s.at[u], dst_ref=low_r.at[u, dy - 1],
-            send_sem=low_send.at[u, dy - 1], recv_sem=low_recv.at[u, dy - 1],
+            src_ref=low_s.at[u, part], dst_ref=low_r.at[u, part, dy - 1],
+            send_sem=low_send.at[u, part, dy - 1], recv_sem=low_recv.at[u, part, dy - 1],
             device_id=(me, lax.rem(y + dy, NY)), device_id_type=MESH,
         )
 
     def base_copy(dy, f):
         hop = dy if dy != 2 else (1, NY - 1)[f]
-        rows = pl.ds(f * (toks // 2), toks // 2)
+        rows = pl.ds(f * (toks // PIECES), toks // PIECES)
         return pltpu.make_async_remote_copy(
             src_ref=base_s.at[dy, rows], dst_ref=base_r.at[dy - 1, rows],
             send_sem=base_send.at[dy - 1, f], recv_sem=base_recv.at[dy - 1, f],
@@ -130,14 +142,17 @@
     def halves(h):
         return FIRST + SECOND if h < HOPS else FIRST
 
-    for name in ("g", "b", "x", "w", "a"):
-        locals_[name].start()
     barrier = pltpu.get_barrier_semaphore()
     partners = [(at(*_xzc(column(k), z)), y) for k in PEERS]
     partners += [(at(x, zplus(d), c), y) for d in DIRS]
     partners += [(me, lax.rem(y + dy, NY)) for dy in range(1, NY)]
     for partner in partners:
         pl.semaphore_signal(barrier, inc=1, device_id=partner, device_id_type=MESH)
+    small = ("table", "gai", "len")
+    for name in small + ("g", "x", "w", "b", "a"):
+        locals_[name].start()
+    for name in small:
+        locals_[name].wait()
 
     ng = gai_ref.shape[1]
     eye = iota((ng, ng), 0) == iota((ng, ng), 1)
@@ -159,7 +174,9 @@
     owner_c = (slot >> 3) & 1
     owner_z = (slot >> 4) & (NZ - 1)
     owner_x = slot >> 7
-    pair = (owner_x * NC + owner_c) * NZ + ((owner_z + (NZ - 2) + (NZ - z)) & (NZ - 1))
+    ahead = (owner_z + (NZ - z)) & (NZ - 1)
+    entry = jnp.maximum(NZ - 1 - 2 * jnp.minimum(ahead, NZ - ahead) + jnp.where(ahead > HOPS, 1, 0), 0)
+    pair = (owner_x * NC + owner_c) * NZ + entry
     start = jnp.sum(jnp.where(iota((ng, ng), 1) < iota((ng, ng), 0), len_row, 0.0), axis=1, keepdims=True)
     shift = (pair * CAP).astype(F32) - start
     end = start + len_col
@@ -184,6 +201,7 @@
 
     for d, f in halves(1):
         ag_copy(0, d, 1, f).start()
+
     for i in range(len(PEERS)):
         meta_copy(i).start()
 
@@ -217,7 +235,7 @@
 
     def base_relay(dy, f):
         base_copy(2, f).wait_recv()
-        rows = pl.ds(f * (toks // 2), toks // 2)
+        rows = pl.ds(f * (toks // PIECES), toks // PIECES)
         base_s[dy, rows, :] = (base_s[dy, rows, :].astype(F32) + base_r[1, rows, :].astype(F32)).astype(BF16)
         base_copy(dy, f).start()
 
@@ -230,26 +248,27 @@
     project_of = (tokg, tokx)
     maps_of = (agb, aga)
 
-    def project(u, first, count):
+    def project(u, part):
+        first, count = LOWS[u][part]
+
         def block(e, carry):
             wide_p = mm(project_of[u][e].reshape(ROWS, -1), maps_of[u][owner_z_of(e)], NT) * masks[e]
             part_low = mm(wide_p.astype(BF16), select(e, False))
-            low_acc[...] = jnp.where(e == 0, part_low, low_acc[...] + part_low)
+            low_acc[...] = jnp.where(e == first, part_low, low_acc[...] + part_low)
             return carry
 
         lax.fori_loop(first, first + count, block, 0)
-
-    def low_sends(u):
-        low_s[u] = low_acc[...].astype(BF16)
+        low_s[u, part] = low_acc[...].astype(BF16)
         for dy in (2, 1, 3):
-            low_copy(u, dy).start()
-
-    def spread(u):
-        total = low_s[u].astype(F32)
+            low_copy(u, part, dy).start()
+
+    def spread(u, part):
+        total = low_s[u, part].astype(F32)
         for dy in range(1, NY):
-            low_copy(u, dy).wait_recv()
-            total = total + low_r[u, dy - 1].astype(F32)
+            low_copy(u, part, dy).wait_recv()
+            total = total + low_r[u, part, dy - 1].astype(F32)
         low = total.astype(BF16)
+        first, count = LOWS[u][part]
 
         def block(e, carry):
             twice = mm(low, select(e, True)) * (2.0 * masks[e])
@@ -258,14 +277,14 @@
             wide_t[u, e] = twice.T.astype(BF16)
             return carry
 
-        lax.fori_loop(0, NZ, block, 0)
+        lax.fori_loop(first, first + count, block, 0)
 
     def lora(distance):
-        e = (distance - 2) % NZ
+        e = entry_of(distance)
         lora_s[e] = mm(wide[e], aga[zplus(distance)]).astype(BF16).reshape(PLANE, CAP, -1)
 
     def term(u, distance, f):
-        e = (distance - 2) % NZ
+        e = entry_of(distance)
         return mm(wide_t[u, e, f * HALF : (f + 1) * HALF, :], toks_of[u][e].reshape(ROWS, -1))
 
     def rs_target(d, h):
@@ -334,63 +353,74 @@
         xx, cc = column(PEERS[i])
         pack(xv, xp, xx * NC + cc)
         token_copy(1, i).start()
-    for i in every:
-        token_copy(2, i).start()
+    for unit in range(2, len(TOKENS)):
+        for i in every:
+            token_copy(unit, i).start()
     forward(0, 3, FIRST)
     for d, f in FIRST:
         ag_copy(1, d, 1, f).start()
     own_tokens(gp, tokg)
+    for i in every:
+        meta_copy(i).wait_recv()
+    for e in range(NZ):
+        masks[e] = jnp.broadcast_to(meta_r[:, e : e + 1, :], (PLANE, CAP, ROWS)).reshape(ROWS, ROWS)
     forward(0, 3, SECOND)
     for d, f in SECOND:
         ag_copy(1, d, 1, f).start()
     own_tokens(xp, tokx)
-    for i in every:
-        meta_copy(i).wait_recv()
-    for e in range(NZ):
-        masks[e] = jnp.broadcast_to(meta_r[:, e : e + 1, :], (PLANE, CAP, ROWS)).reshape(ROWS, ROWS)
     forward(0, HOPS, FIRST)
     locals_["b"].wait()
+
+    def landed(unit):
+        for i in every:
+            token_copy(unit, i).wait_recv()
+
+    landed(0)
+    project(0, 0)
     forward(1, 1, FIRST)
-    for i in every:
-        token_copy(0, i).wait_recv()
-    project(0, 0, NZ // 2)
     forward(1, 1, SECOND)
-    project(0, NZ // 2, NZ // 2)
-    low_sends(0)
+    base_block(0)
+    forward(1, 2, FIRST)
+    landed(2)
+    project(0, 1)
     base_relay(1, 0)
     base_relay(3, 1)
-    forward(1, 2, FIRST)
-    spread(0)
+    locals_["a"].wait()
     forward(1, 2, SECOND)
-    locals_["a"].wait()
-    for distance in (0, 1, -1, 2, -2):
-        lora(distance)
     forward(1, 3, FIRST)
-    for i in every:
-        token_copy(1, i).wait_recv()
     forward(1, 3, SECOND)
+    spread(0, 0)
+    landed(1)
     rs_init(0)
     lora(3)
     lora(-3)
     forward(1, HOPS, FIRST)
     lora(HOPS)
+    spread(0, 1)
+    lora(2)
+    lora(-2)
+    rs_step(0, 1, FIRST)
+    landed(3)
+    project(1, 0)
+    landed(4)
+    project(0, 2)
+    rs_step(0, 2, SECOND)
+    rs_step(0, 2, FIRST)
+    spread(0, 2)
+    for distance in (0, 1, -1):
+        lora(distance)
     for i in every:
         lora_copy(i).start()
     lora_r[pl.ds(p, 1)] = lora_s[:, pl.ds(p, 1)].reshape(1, NZ, CAP, -1)
-    project(1, 0, NEAR)
-    rs_step(0, 1, FIRST)
-    for i in every:
-        token_copy(2, i).wait_recv()
-    rs_step(0, 2, SECOND)
-    project(1, NEAR, NZ - NEAR)
-    low_sends(1)
-    rs_step(0, 2, FIRST)
-    base_block(0)
+    landed(5)
     rs_step(0, 3, SECOND)
-    spread(1)
+    landed(6)
+    project(1, 1)
     rs_step(0, 3, FIRST)
+    spread(1, 0)
     rs_init(1)
     rs_last(0)
+    spread(1, 1)
     rs_step(1, 1, FIRST)
     rs_step(1, 2, SECOND)
     rs_step(1, 2, FIRST)
@@ -398,7 +428,7 @@
     rs_step(1, 3, FIRST)
     for i in every:
         lora_copy(i).wait_recv()
-    for f in (0, 1):
+    for f in range(PIECES):
         for dy in (1, NY - 1):
             base_copy(dy, f).wait_recv()
     lax.fori_loop(0, toks // ROWS, finish, 0)
@@ -406,7 +436,7 @@
 
     for i in range(len(PEERS)):
         meta_copy(i).wait_send()
-        for unit in range(3):
+        for unit in range(len(TOKENS)):
             token_copy(unit, i).wait_send()
         lora_copy(i).wait_send()
     for u in (0, 1):
@@ -418,9 +448,10 @@
                     if h > 1 or f == d:
                         rs_copy(u, d, h, f).wait_send()
         for dy in range(1, NY):
-            low_copy(u, dy).wait_send()
+            for part in range(len(LOWS[u])):
+                low_copy(u, part, dy).wait_send()
     for dy in range(1, NY):
-        for f in (0, 1):
+        for f in range(PIECES):
             base_copy(dy, f).wait_send()
 
 
@@ -459,7 +490,7 @@
             pltpu.VMEM((own, feats), F32),
             pltpu.VMEM((own, feats), F32),
         ),
-        in_specs=[any_spec] * 5 + [vmem_spec] * 3,
+        in_specs=[any_spec] * 8,
         out_specs=(vmem_spec,) * 3,
         scratch_shapes=[
             pltpu.VMEM((toks, feats), BF16),
@@ -475,8 +506,8 @@
             pltpu.VMEM((PLANE, NZ, ROWS), F32),
             pltpu.VMEM((NZ, ROWS, ROWS), F32),
             pltpu.VMEM((ROWS, ROWS), F32),
-            pltpu.VMEM((2, ROWS, ROWS), BF16),
-            pltpu.VMEM((2, NY - 1, ROWS, ROWS), BF16),
+            pltpu.VMEM((2, 3, ROWS, ROWS), BF16),
+            pltpu.VMEM((2, 3, NY - 1, ROWS, ROWS), BF16),
             pltpu.VMEM((NZ, ROWS, ROWS), BF16),
             pltpu.VMEM((2, NZ, ROWS, ROWS), BF16),
             pltpu.VMEM((NY, toks, feats), BF16),
@@ -487,17 +518,20 @@
             pltpu.VMEM((2, 2, HOPS, 2, HALF, feats), BF16),
             pltpu.VMEM((1, toks), jnp.int32),
             pltpu.VMEM((toks, 1), jnp.int32),
-            dma((5,)),
-            dma((5, n)),
-            dma((5, n)),
+            pltpu.VMEM((1, adapter_slot_table.shape[0]), jnp.int32),
+            pltpu.VMEM(group_adapter_index.shape, jnp.int32),
+            pltpu.VMEM(group_token_length.shape, jnp.int32),
+            dma((8,)),
+            dma((len(TOKENS) + 2, n)),
+            dma((len(TOKENS) + 2, n)),
             dma((2, 2, HOPS, 2)),
             dma((2, 2, HOPS, 2)),
             dma((2, 2, HOPS, 2)),
             dma((2, 2, HOPS, 2)),
-            dma((2, NY - 1)),
-            dma((2, NY - 1)),
-            dma((NY - 1, 2)),
-            dma((NY - 1, 2)),
+            dma((2, 3, NY - 1)),
+            dma((2, 3, NY - 1)),
+            dma((NY - 1, PIECES)),
+            dma((NY - 1, PIECES)),
         ],
         compiler_params=pltpu.CompilerParams(
             collective_id=0, has_side_effects=True, vmem_limit_bytes=60 * 1024 * 1024

time: 96.8 us -> 96.4 us (level)
  no operation moved by 1% of the time
where the time goes in v5:
time: 96.4 us; the launch traced here: 95.3 us
  Pallas kernels  94.7 us (98%)
    pallas_call x1, Pallas kernels, on_device(): pl.pallas_call(kernel, out_shape=(pltpu.VMEM((toks, feats), BF16), pltpu....  93.4 us

profile of v5, /device:TPU:8, one launch (start us, length us, event | category | flops | bytes accessed | tf_op | source)
XLA Modules:
  0.0 95.3 jit_solution(2397105391759300171)
XLA Ops:
  0.6 93.4 %lora_backward.1 = (bf16[512,1024]{1,0:T(8,128)(2,1)S(1)}, f32[128,1024]{1,0:T(8,128)S(1)}, f32[128,1024]{1,0:T(8,128)S(1)}) custom-call(bf16[512,1024]{1,0:T(8,128)(2,1)} %x_hbm.1, bf16[512,1024]{1,0:T(8,128)(2,1)} %g_hbm.1, bf16[4096,1024]{1,0:T(8,128)(2,1)} %w_hbm.1, bf16[128,1024]{1,0:T(8,128)(2,1)} %ad_hbm.1, bf16[128,1024]{1,0:T(8,128)(2,1)} %bu_hbm.1, ...), custom_call_target="tpu_custom_call" | custom-call | tf_op jit(solution)/shard_map/lora_backward/pallas_call | solution.py:486
  94.0 1.3 %emit.1 = (bf16[512,1024]{1,0:T(8,128)(2,1)}, f32[128,1024]{1,0:T(8,128)}, f32[128,1024]{1,0:T(8,128)}) custom-call(bf16[512,1024]{1,0:T(8,128)(2,1)S(1)} %get-tuple-element.6.refs_0_, f32[128,1024]{1,0:T(8,128)S(1)} %get-tuple-element.7.refs_1_, f32[128,1024]{1,0:T(8,128)S(1)} %get-tuple-element.8.refs_2_), custom_call_target="tpu_custom_call" | custom-call | tf_op jit(solution)/shard_map/emit/pallas_call | solution.py:550

commit v6 on v5

--- a/solution.py
+++ b/solution.py
@@ -17,7 +17,7 @@
 CAP = 16
 ROWS = PLANE * CAP
 HALF = ROWS // 2
-PEERS = ((2, 0), (2, 1), (1, 0), (1, 1), (3, 0), (3, 1), (0, 1))
+PEERS = ((1, 0), (3, 0), (1, 1), (3, 1), (2, 0), (2, 1), (0, 1))
 DIRS = (1, NZ - 1)
 FIRST, SECOND = ((0, 0), (1, 1)), ((0, 1), (1, 0))
 HOPS = NZ // 2
@@ -327,6 +327,31 @@
         landed[:, pl.ds(p, 1)] = packed[pl.ds(p, 1)].reshape(NZ, 1, CAP, -1)
 
     every = range(len(PEERS))
+
+    def ring_sent(u, hops):
+        for h in hops:
+            for d, f in FIRST + SECOND if h > 1 else FIRST:
+                rs_copy(u, d, h, f).wait_send()
+
+    def plane_sent():
+        for i in every:
+            meta_copy(i).wait_send()
+            for unit in range(len(TOKENS)):
+                token_copy(unit, i).wait_send()
+
+    def gather_sent(u):
+        for h in range(1, HOPS + 1):
+            for d, f in halves(h):
+                ag_copy(u, d, h, f).wait_send()
+
+    def tensor_sent():
+        for dy in range(1, NY):
+            for u in (0, 1):
+                for part in range(len(LOWS[u])):
+                    low_copy(u, part, dy).wait_send()
+            for f in range(PIECES):
+                base_copy(dy, f).wait_send()
+
     locals_["g"].wait()
     for i in every:
         xx, cc = column(PEERS[i])
@@ -420,10 +445,15 @@
     spread(1, 0)
     rs_init(1)
     rs_last(0)
+    gather_sent(0)
+    gather_sent(1)
+    rs_step(1, 1, FIRST)
+    plane_sent()
+    rs_step(1, 2, SECOND)
     spread(1, 1)
-    rs_step(1, 1, FIRST)
-    rs_step(1, 2, SECOND)
+    ring_sent(0, range(1, HOPS + 1))
     rs_step(1, 2, FIRST)
+    tensor_sent()
     rs_step(1, 3, SECOND)
     rs_step(1, 3, FIRST)
     for i in every:
@@ -432,27 +462,12 @@
         for dy in (1, NY - 1):
             base_copy(dy, f).wait_recv()
     lax.fori_loop(0, toks // ROWS, finish, 0)
+    for i in every:
+        lora_copy(i).wait_send()
+    ring_sent(1, range(1, HOPS))
     rs_last(1)
 
-    for i in range(len(PEERS)):
-        meta_copy(i).wait_send()
-        for unit in range(len(TOKENS)):
-            token_copy(unit, i).wait_send()
-        lora_copy(i).wait_send()
-    for u in (0, 1):
-        for h in range(1, HOPS + 1):
-            for d, f in halves(h):
-                ag_copy(u, d, h, f).wait_send()
-            for f in (0, 1):
-                for d in (0, 1):
-                    if h > 1 or f == d:
-                        rs_copy(u, d, h, f).wait_send()
-        for dy in range(1, NY):
-            for part in range(len(LOWS[u])):
-                low_copy(u, part, dy).wait_send()
-    for dy in range(1, NY):
-        for f in range(PIECES):
-            base_copy(dy, f).wait_send()
+    ring_sent(1, (HOPS,))
 
 
 def _xzc(xc, z):

time: 96.4 us -> 95.2 us (0.988)
  no operation moved by 1% of the time
where the time goes in v6:
time: 95.2 us; the launch traced here: 95.1 us
  Pallas kernels  94.5 us (99%)
    pallas_call x1, Pallas kernels, on_device(): pl.pallas_call(kernel, out_shape=(pltpu.VMEM((toks, feats), BF16), pltpu....  93.1 us

profile of v6, /device:TPU:8, one launch (start us, length us, event | category | flops | bytes accessed | tf_op | source)
XLA Modules:
  0.0 95.1 jit_solution(2324090355219739389)
XLA Ops:
  0.6 93.1 %lora_backward.1 = (bf16[512,1024]{1,0:T(8,128)(2,1)S(1)}, f32[128,1024]{1,0:T(8,128)S(1)}, f32[128,1024]{1,0:T(8,128)S(1)}) custom-call(bf16[512,1024]{1,0:T(8,128)(2,1)} %x_hbm.1, bf16[512,1024]{1,0:T(8,128)(2,1)} %g_hbm.1, bf16[4096,1024]{1,0:T(8,128)(2,1)} %w_hbm.1, bf16[128,1024]{1,0:T(8,128)(2,1)} %ad_hbm.1, bf16[128,1024]{1,0:T(8,128)(2,1)} %bu_hbm.1, ...), custom_call_target="tpu_custom_call" | custom-call | tf_op jit(solution)/shard_map/lora_backward/pallas_call | solution.py:501
  93.8 1.3 %emit.1 = (bf16[512,1024]{1,0:T(8,128)(2,1)}, f32[128,1024]{1,0:T(8,128)}, f32[128,1024]{1,0:T(8,128)}) custom-call(bf16[512,1024]{1,0:T(8,128)(2,1)S(1)} %get-tuple-element.6.refs_0_, f32[128,1024]{1,0:T(8,128)S(1)} %get-tuple-element.7.refs_1_, f32[128,1024]{1,0:T(8,128)S(1)} %get-tuple-element.8.refs_2_), custom_call_target="tpu_custom_call" | custom-call | tf_op jit(solution)/shard_map/emit/pallas_call | solution.py:565
